TPU v7x, 32 devices: a whole 2x2x4 slice. The times are simulated.
32 devices in a mesh: group: 2 (over y), seq: 4 (over z), chan: 2 (over x), sub: 2 (over core).
Axes of the slice: x: 2, y: 2, z: 4, core: 2. Of those that a mesh axis runs over, the one named last changes fastest.
Arguments:
- atom_single: bfloat16 [12288, 128], P(('group', 'seq', 'chan', 'sub')), parts along dimension 0, may hold values from -6 to 6
- atom_token: int32 [12288], P(('group', 'seq', 'chan', 'sub')), parts along dimension 0, may hold values from 0 to 767, as said below
- token_atoms: int32 [1536], P(('group', 'seq', 'chan', 'sub')), parts along dimension 0, may hold values from 1 to 19, as said below
- window_offset: int32 [384], P(('group', 'seq', 'chan', 'sub')), parts along dimension 0, may hold values from 0 to 96
- token_pair: bfloat16 [1536, 64, 128], P(('group', 'seq', 'chan', 'sub')), parts along dimension 0, may hold values from -6 to 6
- w_zpair: bfloat16 [128, 16], replicated, may hold values from -0.5 to 0.5
- w_single: bfloat16 [2, 128, 16], replicated, may hold values from -0.5 to 0.5
- w_pair_mlp: bfloat16 [3, 16, 16], replicated, may hold values from -1.5 to 1.5
- w_bias: bfloat16 [3, 16, 4], replicated, may hold values from -1.5 to 1.5
- w_attn: bfloat16 [3, 4, 128, 128], replicated, may hold values from -0.5 to 0.5
- w_out: bfloat16 [3, 128, 128], replicated, may hold values from -0.5 to 0.5
- w_trans_in: bfloat16 [3, 2, 128, 256], replicated, may hold values from -0.5 to 0.5
- w_trans_out: bfloat16 [3, 256, 128], replicated, may hold values from -0.375 to 0.375
- w_token: bfloat16 [128, 768], replicated, may hold values from -0.5 to 0.5
Outputs:
- token_single: bfloat16 [1536, 768], P(('group', 'seq', 'chan', 'sub')), parts along dimension 0
- atom_out: bfloat16 [12288, 128], P(('group', 'seq', 'chan', 'sub')), parts along dimension 0
There are 2 independent parts, one for each index of `group`. A program takes and returns all parts, laid end to end along the dimension named above; an argument that names none is the same for every part. Nothing has to cross between parts.
Inputs may be any that keep to these rules, and one draw needn't show every extreme that they name: atom_token is non-decreasing and gives each token t exactly token_atoms[t] consecutive atoms. `token_atoms`: the atoms of the first aligned block of 48 tokens begin at 0; those of every later block s begin 384 // 8 to 96 atoms after 384 s; all tokens together have 6144 atoms.
All inputs are finite; a program needn't handle non-finite values.
Results may differ from a plain program's by a relative error of at most 0.01.
Values may be sent and summed in bfloat16 or wider, within the bound.
No kernel may reach another device: no remote copies, remote signals or barrier semaphores. Data moves between devices by JAX's collectives and lax.ppermute only.
A program may use at most 64 MiB of HBM per device.

v0:
```python
import math

import jax
import jax.numpy as jnp
from jax import lax
from jax.sharding import PartitionSpec as P

BLOCKS = 3
QB = 32
KW = 128
HALO = 96


EPSILON = 1e-05


def padded_2(x, sides, width):
    for axis, dim in sides:
        size, length = (lax.axis_size(axis), x.shape[dim])
        up = [(i, (i + 1) % size) for i in range(size - 1)]
        down = [(j, i) for i, j in up]
        last = lax.slice_in_dim(x, length - width, length, axis=dim)
        leading = lax.slice_in_dim(x, 0, width, axis=dim)
        before = lax.ppermute(last, axis, up)
        after = lax.ppermute(leading, axis, down)
        x = jnp.concatenate([before, x, after], axis=dim)
    return x


def passed_along(block, axis, distance):
    devices = range(lax.axis_size(axis))
    route = [(i - distance, i) for i in devices if i - distance in devices]
    return lax.ppermute(block, axis, route)


def normalize(values, axis):
    centre = jnp.mean(values, axis=axis, keepdims=True)
    shifted = values - centre
    spread = jnp.mean(shifted * shifted, axis=axis, keepdims=True)
    return shifted * lax.rsqrt(spread + EPSILON)


def project_rows(rows, w_zpair):
    normed_rows = normalize(rows.astype(jnp.float32), 2).astype(jnp.bfloat16)
    projected = jnp.einsum(
        "twc,ce->etw", normed_rows, w_zpair, preferred_element_type=jnp.float32
    ).astype(jnp.bfloat16)
    return projected.reshape(projected.shape[0], projected.shape[1] * projected.shape[2])


def window_halo(values):
    return padded_2(values, ((("seq", "chan", "sub"), 0),), HALO)


def pair_bias(pair_start, w_pair_mlp, w_bias):
    high = lax.Precision.HIGHEST
    mlp_f = w_pair_mlp.astype(jnp.float32)
    first = jnp.einsum("enqk,ef->fnqk", jax.nn.relu(pair_start), mlp_f[0], precision=high)
    second = jnp.einsum("enqk,ef->fnqk", jax.nn.relu(first), mlp_f[1], precision=high)
    third = jnp.einsum("enqk,ef->fnqk", jax.nn.relu(second), mlp_f[2], precision=high)
    pair = pair_start + third
    return jnp.einsum(
        "enqk,leh->lhnqk", normalize(pair, 0), w_bias.astype(jnp.float32), precision=high
    )


def shards(
    atom_single,
    atom_token,
    token_atoms,
    window_offset,
    token_pair,
    w_zpair,
    w_single,
    w_pair_mlp,
    w_bias,
    w_attn,
    w_out,
    w_trans_in,
    w_trans_out,
    w_token,
):
    shard_index = lax.axis_index(("seq", "chan", "sub"))
    shard_count = lax.axis_size(("seq", "chan", "sub"))
    atom_rows = atom_single.shape[0]
    token_rows = token_atoms.shape[0]
    width = atom_single.shape[1]
    heads = w_bias.shape[2]
    head_size = width // heads
    windows = atom_rows // QB
    band_width = token_pair.shape[1]
    pair_width = w_zpair.shape[1]
    left_raw = passed_along(token_pair, ("seq", "chan", "sub"), 1)
    flat_band = project_rows(jnp.concatenate([left_raw, token_pair], axis=0), w_zpair)
    relu_single = jnp.maximum(atom_single, jnp.zeros((), atom_single.dtype))
    query_term = jnp.dot(relu_single, w_single[0], preferred_element_type=jnp.float32)
    key_term = jnp.dot(relu_single, w_single[1], preferred_element_type=jnp.float32).astype(
        jnp.bfloat16
    )
    padded_tokens = padded_2(atom_token, ((("seq", "chan", "sub"), 0),), HALO)
    offsets = jnp.arange(KW, dtype=jnp.int32)
    local_start = QB * jnp.arange(windows, dtype=jnp.int32) + window_offset
    key_rows = local_start[:, None] + offsets[None, :]
    global_key = shard_index * atom_rows - HALO + key_rows
    valid = ((global_key >= 0) & (global_key < shard_count * atom_rows)).astype(jnp.float32)
    key_tokens = padded_tokens[key_rows]
    query_tokens = atom_token.reshape(windows, QB)
    row_index = query_tokens - (shard_index - 1) * token_rows
    column = jnp.clip(
        key_tokens[:, None, :] - query_tokens[:, :, None] + band_width // 2, 0, band_width - 1
    )
    flat_index = row_index[:, :, None] * band_width + column
    gathered = jnp.take(flat_band, flat_index.reshape(-1), axis=1).reshape(
        pair_width, windows, QB, KW
    )
    act = atom_single.astype(jnp.float32)
    bias = None
    for layer_index in range(BLOCKS):
        normed = normalize(act, 1).astype(jnp.bfloat16)
        merged_weight = jnp.transpose(w_attn[layer_index], (1, 0, 2)).reshape(width, 4 * width)
        projected = jnp.dot(normed, merged_weight, preferred_element_type=jnp.float32)
        queries = projected[:, :width].astype(jnp.bfloat16)
        keyvals = projected[:, width : 3 * width].astype(jnp.bfloat16)
        gate_logit = projected[:, 3 * width :]
        if layer_index == 0:
            padded = window_halo(jnp.concatenate([keyvals, key_term], axis=1))
            key_side = padded[key_rows][:, :, 2 * width :]
            side_terms = jnp.transpose(key_side, (2, 0, 1))[:, :, None, :].astype(jnp.float32)
            query_side = jnp.transpose(query_term).reshape(pair_width, windows, QB, 1)
            pair_start = gathered.astype(jnp.float32) + query_side + side_terms
            bias = pair_bias(pair_start, w_pair_mlp, w_bias)
        else:
            padded = window_halo(keyvals)
        window_kv = padded[key_rows]
        window_keys = window_kv[:, :, :width].reshape(windows, KW, heads, head_size)
        window_values = window_kv[:, :, width : 2 * width].reshape(windows, KW, heads, head_size)
        query_heads = queries.reshape(windows, QB, heads, head_size)
        scores = (
            jnp.einsum(
                "nqhd,nkhd->hnqk", query_heads, window_keys, preferred_element_type=jnp.float32
            )
            / math.sqrt(head_size)
            + bias[layer_index]
        )
        weights = jnp.exp(scores) * valid[None, :, None, :]
        weights = (weights / jnp.sum(weights, axis=3, keepdims=True)).astype(jnp.bfloat16)
        attended = jnp.einsum(
            "hnqk,nkhd->nqhd", weights, window_values, preferred_element_type=jnp.float32
        ).reshape(atom_rows, width)
        gated = (attended * jax.nn.sigmoid(gate_logit)).astype(jnp.bfloat16)
        act = act + jnp.dot(gated, w_out[layer_index], preferred_element_type=jnp.float32)
        normed_two = normalize(act, 1).astype(jnp.bfloat16)
        joined_weight = jnp.concatenate(
            [w_trans_in[layer_index, 0], w_trans_in[layer_index, 1]], axis=1
        )
        both_parts = jnp.dot(normed_two, joined_weight, preferred_element_type=jnp.float32)
        hidden_width = w_trans_in.shape[3]
        hidden_units = (
            jax.nn.silu(both_parts[:, :hidden_width]) * both_parts[:, hidden_width:]
        ).astype(jnp.bfloat16)
        act = act + jnp.dot(
            hidden_units, w_trans_out[layer_index], preferred_element_type=jnp.float32
        )
    atom_out = act.astype(jnp.bfloat16)
    features = jax.nn.relu(jnp.dot(atom_out, w_token, preferred_element_type=jnp.float32))
    local_token = atom_token - (shard_index - 1) * token_rows
    member = (jnp.arange(2 * token_rows, dtype=jnp.int32)[:, None] == local_token[None, :]).astype(
        jnp.float32
    )
    sums = jnp.dot(member, features, precision=lax.Precision.HIGHEST)
    spill = passed_along(sums[:token_rows].astype(jnp.bfloat16), ("seq", "chan", "sub"), -1).astype(
        jnp.float32
    )
    total = sums[token_rows:] + spill
    token_single = (total / token_atoms[:, None].astype(jnp.float32)).astype(jnp.bfloat16)
    return (token_single, atom_out)


def solution(mesh):
    in_specs = (
        P(("group", "seq", "chan", "sub"), None),
        P(("group", "seq", "chan", "sub")),
        P(("group", "seq", "chan", "sub")),
        P(("group", "seq", "chan", "sub")),
        P(("group", "seq", "chan", "sub"), None, None),
        P(),
        P(),
        P(),
        P(),
        P(),
        P(),
        P(),
        P(),
        P(),
    )
    out_specs = (P(("group", "seq", "chan", "sub"), None), P(("group", "seq", "chan", "sub"), None))
    return jax.shard_map(shards, mesh=mesh, in_specs=in_specs, out_specs=out_specs, check_vma=False)
```

profile of v0, /device:TPU:1, one launch (start us, length us, event | category | flops | bytes accessed | tf_op | source)
XLA Modules:
  0.0 303.0 jit_solution(5069149968193555124)
XLA Ops:
  1.9 1.7 fusion.170
  6.0 4.5 %collective-permute-start = (bf16[96,272]{1,0:T(8,128)(2,1)}, bf16[96,272]{1,0:T(8,128)(2,1)S(1)}, u32[]{:S(2)}, u32[]{:S(2)}) collective-permute-start(bf16[96,272]{1,0:T(8,128)(2,1)} %get-tuple-element.27), channel_id=1, source_target_pairs={{0,1},{1,2},{2,3},{3,4},{4,5},{5,6},{6,7},{7,8},{8,9},{9,10},{10,1... | collective-permute-start | bytes 156680 | tf_op jit(solution)/shard_map/ppermute | solution.py:24
  10.5 1.9 collective-permute-start.1
  12.5 3.6 %collective-permute-start.2 = (s32[96]{0:T(128)S(1)}, s32[96]{0:T(128)S(1)}, u32[]{:S(2)}, u32[]{:S(2)}) collective-permute-start(s32[96]{0:T(128)S(1)} %get-tuple-element.29), channel_id=1, source_target_pairs={{0,1},{1,2},{2,3},{3,4},{4,5},{5,6},{6,7},{7,8},{8,9},{9,10},{10,1... | collective-permute-start | bytes 1160 | tf_op jit(solution)/shard_map/ppermute | solution.py:24
  16.1 1.9 collective-permute-start.3
  18.1 3.6 %collective-permute-start.4 = (bf16[48,64,128]{2,1,0:T(8,128)(2,1)S(1)}, bf16[48,64,128]{2,1,0:T(8,128)(2,1)S(1)}, u32[]{:S(2)}, u32[]{:S(2)}) collective-permute-start(bf16[48,64,128]{2,1,0:T(8,128)(2,1)S(1)} %copy-done.1), channel_id=1, source_target_pairs={{0,1},{1,2},{2,3},{3,4},{4,5},{5,6},{6,7},{7,8},{8,9},{9,10},{10,1... | collective-permute-start | bytes 2359304 | tf_op jit(solution)/shard_map/ppermute | solution.py:33
  26.3 5.8 %gather_fusion.1 = s32[1536]{0:T(1024)S(1)} fusion(s32[576]{0:T(1024)S(1)} %pad_add_fusion, s32[2048]{0:T(1024)S(1)} %pad_clamp_fusion), kind=kCustom, calls=%fused_computation.1 | custom fusion | bytes 18432 | tf_op jit(solution)/shard_map/gather | solution.py:106
  33.5 4.7 %gather_fusion = bf16[1536,272]{1,0:T(8,128)(2,1)S(1)} fusion(bf16[576,272]{1,0:T(8,128)(2,1)S(1)} %pad_maximum_fusion.2, s32[2048]{0:T(1024)S(1)} %pad_clamp_fusion), kind=kCustom, calls=%fused_computation | custom fusion | bytes 1677312 | tf_op jit(solution)/shard_map/gather | solution.py:134
  40.7 1.9 copy.122
  43.8 2.0 fusion.2
  45.9 2.8 fusion.40
  49.5 170.8 %gather_fusion.2 = bf16[49152,16]{1,0:T(8,128)(2,1)} fusion(bf16[16,6144]{0,1:T(8,128)(2,1)S(1)} %bitcast.196, s32[49152]{0:T(1024)S(1)} %copy-done.7), kind=kCustom, calls=%fused_computation.2 | custom fusion | bytes 3342336 | tf_op jit(solution)/shard_map/jit(_take)/gather | solution.py:113
  220.2 9.9 %copy.82 = bf16[49152,16]{0,1:T(8,128)(2,1)S(1)} copy(bf16[49152,16]{1,0:T(8,128)(2,1)} %gather_fusion.2) | data formatting | bytes 3145728 | tf_op jit(solution)/shard_map/jit(_take)/gather | solution.py:113
  232.0 3.8 %fusion.5 = f32[2,8,384,128]{3,1,2,0:T(8,128)S(1)} fusion(f32[2,8,384,128]{3,2,1,0:T(8,128)S(1)} %bitcast.198, f32[2,8,384,128]{3,2,1,0:T(8,128)S(1)} %bitcast.199, bf16[49152,16]{0,1:T(8,128)(2,1)S(1)} %copy.82, pred[49152]{0:T(1024)(128)(4,1)S(1)} %bitcast.219), kind=kLoop, calls=%fused_computation.13 | loop fusion | flops 3932160 | bytes 11059200
  236.5 3.5 %fusion.12 = f32[12,32,128,16]{2,3,1,0:T(8,128)S(1)} fusion(f32[16,12,32,128]{3,2,1,0:T(8,128)S(1)} %bitcast.200, bf16[3,16,16]{2,1,0:T(8,128)(2,1)S(1)} %copy-done.22), kind=kOutput, calls=%fused_computation.22 | convolution fusion | flops 150994944 | bytes 6295552 | tf_op jit(solution)/shard_map/enqk,ef->fnqk/dot_general | solution.py:58
  240.1 1.7 fusion.10
  242.8 3.4 %fusion.174 = (f32[12,32,128]{2,1,0:T(8,128)S(1)}, f32[16,12,32,128]{3,0,2,1:T(8,128)S(1)}) fusion(bf16[3,16,16]{2,1,0:T(8,128)(2,1)S(1)} %copy-done.22, f32[12,32,128,16]{2,3,1,0:T(8,128)S(1)} %fusion.10, f32[16,12,128]{2,0,1:T(8,128)S(1)} %copy-done.6, f32[16,12,32]{0,2,1:T(8,128)S(1)} %bitcast.210, bf16[16,12,32,128]{3,2,1,0:T(8,128)(2,1)S(1)} %bitcast.201, ...), kind=kOutput, calls=%fused_computation.257 | convolution fusion | flops 156450816 | bytes 8409088 | tf_op jit(solution)/shard_map/enqk,ef->fnqk/dot_general | solution.py:60
  247.3 2.2 fusion.6
  250.5 2.4 divide_convert_fusion.2
  252.8 1.4 convolution_bitcast_fusion.2
  258.0 2.7 collective-permute-start.5
  260.8 1.9 collective-permute-start.6
  263.1 4.0 %collective-permute-done.6 = bf16[96,256]{1,0:T(8,128)(2,1)S(1)} collective-permute-done((bf16[96,256]{1,0:T(8,128)(2,1)S(1)}, bf16[96,256]{1,0:T(8,128)(2,1)S(1)}, u32[]{:S(2)}, u32[]{:S(2)}) %collective-permute-start.6) | collective-permute-done | bytes 49184 | tf_op jit(solution)/shard_map/ppermute | solution.py:25
  267.1 4.8 %gather_fusion.3 = bf16[1536,256]{1,0:T(8,128)(2,1)S(1)} fusion(bf16[576,256]{1,0:T(8,128)(2,1)S(1)} %pad_maximum_fusion.3, s32[2048]{0:T(1024)S(1)} %pad_clamp_fusion), kind=kCustom, calls=%fused_computation.3 | custom fusion | bytes 1579008 | tf_op jit(solution)/shard_map/gather | solution.py:134
  272.5 1.6 divide_convert_fusion.1
  277.3 1.9 collective-permute-start.7
  279.2 2.4 collective-permute-start.8
  281.9 3.6 %collective-permute-done.8 = bf16[96,256]{1,0:T(8,128)(2,1)S(1)} collective-permute-done((bf16[96,256]{1,0:T(8,128)(2,1)S(1)}, bf16[96,256]{1,0:T(8,128)(2,1)S(1)}, u32[]{:S(2)}, u32[]{:S(2)}) %collective-permute-start.8) | collective-permute-done | bytes 49184 | tf_op jit(solution)/shard_map/ppermute | solution.py:25
  285.6 5.0 %gather_fusion.4 = bf16[1536,256]{1,0:T(8,128)(2,1)S(1)} fusion(bf16[576,256]{1,0:T(8,128)(2,1)S(1)} %pad_maximum_fusion.4, s32[2048]{0:T(1024)S(1)} %pad_clamp_fusion), kind=kCustom, calls=%fused_computation.4 | custom fusion | bytes 1579008 | tf_op jit(solution)/shard_map/gather | solution.py:134
  291.3 1.6 divide_convert_fusion
  296.6 1.9 collective-permute-start.9
  299.3 3.0 collective-permute-done.9
  (174 shorter events, 33.2 us)
Async XLA Ops:
  0.6 295.0 %copy-start = (bf16[128,768]{1,0:T(8,128)(2,1)S(1)}, bf16[128,768]{1,0:T(8,128)(2,1)}, u32[]{:S(2)}) copy-start(bf16[128,768]{1,0:T(8,128)(2,1)} %param.27) | copy-start | bytes 589828
  0.6 4.4 %copy-start.14 = (bf16[384,128]{1,0:T(8,128)(2,1)S(1)}, bf16[384,128]{1,0:T(8,128)(2,1)}, u32[]{:S(2)}) copy-start(bf16[384,128]{1,0:T(8,128)(2,1)} %param.14) | copy-start | bytes 294916
  0.7 4.4 %copy-start.25 = (bf16[2,128,16]{1,2,0:T(8,128)(2,1)S(1)}, bf16[2,128,16]{1,2,0:T(8,128)(2,1)}, u32[]{:S(2)}) copy-start(bf16[2,128,16]{1,2,0:T(8,128)(2,1)} %param.20) | copy-start | bytes 24580
  0.7 11.8 %copy-start.21 = (s32[384]{0:T(512)S(1)}, s32[384]{0:T(512)}, u32[]{:S(2)}) copy-start(s32[384]{0:T(512)} %param.15) | copy-start | bytes 4612
  0.7 17.4 %copy-start.1 = (bf16[48,64,128]{2,1,0:T(8,128)(2,1)S(1)}, bf16[48,64,128]{2,1,0:T(8,128)(2,1)}, u32[]{:S(2)}) copy-start(bf16[48,64,128]{2,1,0:T(8,128)(2,1)} %param.18) | copy-start | bytes 2359300
  0.7 21.3 %copy-start.28 = (s32[12]{0:T(128)S(1)}, s32[12]{0:T(128)}, u32[]{:S(2)}) copy-start(s32[12]{0:T(128)} %param.17) | copy-start | bytes 148
  0.7 22.0 %copy-start.12 = (bf16[3,2,128,256]{3,2,1,0:T(8,128)(2,1)S(1)}, bf16[3,2,128,256]{3,2,1,0:T(8,128)(2,1)}, u32[]{:S(2)}) copy-start(bf16[3,2,128,256]{3,2,1,0:T(8,128)(2,1)} %param.25) | copy-start | bytes 1179652
  6.0 27.4 %collective-permute-start = (bf16[96,272]{1,0:T(8,128)(2,1)}, bf16[96,272]{1,0:T(8,128)(2,1)S(1)}, u32[]{:S(2)}, u32[]{:S(2)}) collective-permute-start(bf16[96,272]{1,0:T(8,128)(2,1)} %get-tuple-element.27), channel_id=1, source_target_pairs={{0,1},{1,2},{2,3},{3,4},{4,5},{5,6},{6,7},{7,8},{8,9},{9,10},{10,1... | collective-permute-start | bytes 156680 | tf_op jit(solution)/shard_map/ppermute | solution.py:24
  10.5 22.9 %collective-permute-start.1 = (bf16[96,272]{1,0:T(8,128)(2,1)}, bf16[96,272]{1,0:T(8,128)(2,1)S(1)}, u32[]{:S(2)}, u32[]{:S(2)}) collective-permute-start(bf16[96,272]{1,0:T(8,128)(2,1)} %get-tuple-element.28), channel_id=1, source_target_pairs={{1,0},{2,1},{3,2},{4,3},{5,4},{6,5},{7,6},{8,7},{9,8},{10,9},{11,1... | collective-permute-start | bytes 156680 | tf_op jit(solution)/shard_map/ppermute | solution.py:25
  12.5 13.7 %collective-permute-start.2 = (s32[96]{0:T(128)S(1)}, s32[96]{0:T(128)S(1)}, u32[]{:S(2)}, u32[]{:S(2)}) collective-permute-start(s32[96]{0:T(128)S(1)} %get-tuple-element.29), channel_id=1, source_target_pairs={{0,1},{1,2},{2,3},{3,4},{4,5},{5,6},{6,7},{7,8},{8,9},{9,10},{10,1... | collective-permute-start | bytes 1160 | tf_op jit(solution)/shard_map/ppermute | solution.py:24
  16.1 10.0 %collective-permute-start.3 = (s32[96]{0:T(128)S(1)}, s32[96]{0:T(128)S(1)}, u32[]{:S(2)}, u32[]{:S(2)}) collective-permute-start(s32[96]{0:T(128)S(1)} %get-tuple-element.30), channel_id=1, source_target_pairs={{1,0},{2,1},{3,2},{4,3},{5,4},{6,5},{7,6},{8,7},{9,8},{10,9},{11,1... | collective-permute-start | bytes 1160 | tf_op jit(solution)/shard_map/ppermute | solution.py:25
  18.1 24.8 %collective-permute-start.4 = (bf16[48,64,128]{2,1,0:T(8,128)(2,1)S(1)}, bf16[48,64,128]{2,1,0:T(8,128)(2,1)S(1)}, u32[]{:S(2)}, u32[]{:S(2)}) collective-permute-start(bf16[48,64,128]{2,1,0:T(8,128)(2,1)S(1)} %copy-done.1), channel_id=1, source_target_pairs={{0,1},{1,2},{2,3},{3,4},{4,5},{5,6},{6,7},{7,8},{8,9},{9,10},{10,1... | collective-permute-start | bytes 2359304 | tf_op jit(solution)/shard_map/ppermute | solution.py:33
  23.7 8.5 %copy-start.3 = (f32[16,384]{0,1:T(8,128)}, f32[16,384]{0,1:T(8,128)S(1)}, u32[]{:S(2)}) copy-start(f32[16,384]{0,1:T(8,128)S(1)} %copy.118) | copy-start | bytes 73732
  39.8 6.1 %copy-start.27 = (bf16[128,16]{0,1:T(8,128)(2,1)S(1)}, bf16[128,16]{0,1:T(8,128)(2,1)}, u32[]{:S(2)}) copy-start(bf16[128,16]{0,1:T(8,128)(2,1)} %param.19) | copy-start | bytes 12292
  45.8 3.6 %copy-start.7 = (s32[49152]{0:T(1024)S(1)}, s32[49152]{0:T(1024)}, u32[]{:S(2)}) copy-start(s32[49152]{0:T(1024)} %broadcast_clamp_fusion) | copy-start | bytes 589828
  220.2 10.0 %copy-start.8 = (f32[16,12,128]{2,1,0:T(8,128)S(1)}, f32[16,12,128]{2,1,0:T(8,128)}, u32[]{:S(2)}) copy-start(f32[16,12,128]{2,1,0:T(8,128)} %copy.134) | copy-start | bytes 294916
  246.2 1.1 copy-start.24
  249.8 3.0 copy-start.2
  252.8 3.3 %copy-start.19 = (bf16[128,256]{1,0:T(8,128)(2,1)S(1)}, bf16[128,256]{1,0:T(8,128)(2,1)}, u32[]{:S(2)}) copy-start(bf16[128,256]{1,0:T(8,128)(2,1)} %get-tuple-element.17) | copy-start | bytes 196612
  252.8 3.4 %copy-start.20 = (bf16[128,256]{1,0:T(8,128)(2,1)S(1)}, bf16[128,256]{1,0:T(8,128)(2,1)}, u32[]{:S(2)}) copy-start(bf16[128,256]{1,0:T(8,128)(2,1)} %get-tuple-element.18) | copy-start | bytes 196612
  254.5 3.2 %copy-start.9 = (bf16[1,4,128,128]{2,3,1,0:T(8,128)(2,1)S(1)}, bf16[1,4,128,128]{2,3,1,0:T(8,128)(2,1)}, u32[]{:S(2)}) copy-start(bf16[1,4,128,128]{2,3,1,0:T(8,128)(2,1)} %copy.127) | copy-start | bytes 393220
  254.9 7.8 %copy-start.11 = (bf16[1,4,128,128]{3,2,1,0:T(8,128)(2,1)S(1)}, bf16[1,4,128,128]{3,2,1,0:T(8,128)(2,1)}, u32[]{:S(2)}) copy-start(bf16[1,4,128,128]{3,2,1,0:T(8,128)(2,1)} %get-tuple-element.22) | copy-start | bytes 393220
  258.0 5.1 %collective-permute-start.5 = (bf16[96,256]{1,0:T(8,128)(2,1)S(1)}, bf16[96,256]{1,0:T(8,128)(2,1)S(1)}, u32[]{:S(2)}, u32[]{:S(2)}) collective-permute-start(bf16[96,256]{1,0:T(8,128)(2,1)S(1)} %get-tuple-element.25), channel_id=1, source_target_pairs={{0,1},{1,2},{2,3},{3,4},{4,5},{5,6},{6,7},{7,8},{8,9},{9,10},{10,1... | collective-permute-start | bytes 147464 | tf_op jit(solution)/shard_map/ppermute | solution.py:24
  260.8 6.3 %collective-permute-start.6 = (bf16[96,256]{1,0:T(8,128)(2,1)S(1)}, bf16[96,256]{1,0:T(8,128)(2,1)S(1)}, u32[]{:S(2)}, u32[]{:S(2)}) collective-permute-start(bf16[96,256]{1,0:T(8,128)(2,1)S(1)} %get-tuple-element.26), channel_id=1, source_target_pairs={{1,0},{2,1},{3,2},{4,3},{5,4},{6,5},{7,6},{8,7},{9,8},{10,9},{11,1... | collective-permute-start | bytes 147464 | tf_op jit(solution)/shard_map/ppermute | solution.py:25
  274.1 1.4 copy-start.17
  274.1 1.4 copy-start.18
  277.3 4.6 %collective-permute-start.7 = (bf16[96,256]{1,0:T(8,128)(2,1)S(1)}, bf16[96,256]{1,0:T(8,128)(2,1)S(1)}, u32[]{:S(2)}, u32[]{:S(2)}) collective-permute-start(bf16[96,256]{1,0:T(8,128)(2,1)S(1)} %get-tuple-element.20), channel_id=1, source_target_pairs={{0,1},{1,2},{2,3},{3,4},{4,5},{5,6},{6,7},{7,8},{8,9},{9,10},{10,1... | collective-permute-start | bytes 147464 | tf_op jit(solution)/shard_map/ppermute | solution.py:24
  279.2 6.3 %collective-permute-start.8 = (bf16[96,256]{1,0:T(8,128)(2,1)S(1)}, bf16[96,256]{1,0:T(8,128)(2,1)S(1)}, u32[]{:S(2)}, u32[]{:S(2)}) collective-permute-start(bf16[96,256]{1,0:T(8,128)(2,1)S(1)} %get-tuple-element.21), channel_id=1, source_target_pairs={{1,0},{2,1},{3,2},{4,3},{5,4},{6,5},{7,6},{8,7},{9,8},{10,9},{11,1... | collective-permute-start | bytes 147464 | tf_op jit(solution)/shard_map/ppermute | solution.py:25
  292.9 1.4 copy-start.15
  292.9 1.4 copy-start.16
  294.2 4.3 %copy-start.29 = (s32[48]{0:T(128)S(1)}, s32[48]{0:T(128)}, u32[]{:S(2)}) copy-start(s32[48]{0:T(128)} %param.16) | copy-start | bytes 580
  296.6 5.7 %collective-permute-start.9 = (bf16[48,768]{1,0:T(8,128)(2,1)S(1)}, bf16[48,768]{1,0:T(8,128)(2,1)S(1)}, u32[]{:S(2)}, u32[]{:S(2)}) collective-permute-start(bf16[48,768]{1,0:T(8,128)(2,1)S(1)} %slice.391), channel_id=1, source_target_pairs={{1,0},{2,1},{3,2},{4,3},{5,4},{6,5},{7,6},{8,7},{9,8},{10,9},{11,1... | collective-permute-start | bytes 221192 | tf_op jit(solution)/shard_map/ppermute | solution.py:33
  (8 other events, 7.2 us)
where the time goes:
time: 305 us; the launch traced here: 303 us
  local copies, waits for them, and re-layouts  222 us (73%)
  matrix products  30 us (10%)
  starting transfers between devices  26.5 us (9%)
  other arithmetic  11.8 us (4%)
  waiting for transfers between devices  10.6 us (3%)
    gather x2, local copies, waits for them, and re-layouts, shards(): jnp.take(flat_band, flat_index.reshape(-1), axis=1)  181 us
    gather x3, local copies, waits for them, and re-layouts, shards(): window_kv = padded[key_rows]  14.5 us
    ppermute x4, starting transfers between devices, padded_2(): before = lax.ppermute(last, axis, up)  12.8 us
    unnamed x76, local copies, waits for them, and re-layouts  11.3 us
    ppermute x4, starting transfers between devices, padded_2(): after = lax.ppermute(leading, axis, down)  8.17 us
    ppermute x4, waiting for transfers between devices, padded_2(): after = lax.ppermute(leading, axis, down)  7.6 us
  transfers between devices with their start and end apart: 10, of which 3 were waited for; matrix products, arithmetic and copies ran while one was open for 7% of the time, Pallas kernels for 0%

commit v1 on v0

v1 whole, which is shorter than its diff:
```python
import functools
import math

import jax
import jax.numpy as jnp
from jax import lax
from jax.experimental import pallas as pl
from jax.experimental.pallas import tpu as pltpu
from jax.sharding import PartitionSpec as P

BLOCKS = 3
QB = 32
KW = 128
HALO = 96
LANES = 128
CHUNK = 3
EPSILON = 1e-05
RING = ("seq", "chan", "sub")
NT = (((1,), (1,)), ((), ()))
F32 = jnp.float32
BF16 = jnp.bfloat16


def dot(a, b):
    return jnp.dot(a, b, preferred_element_type=F32)


def dot_nt(a, b):
    return lax.dot_general(a, b, NT, preferred_element_type=F32)


def iota(shape, axis):
    return lax.broadcasted_iota(jnp.int32, shape, axis)


def shard_place():
    index, count = 0, 1
    for name in RING:
        index = index * lax.axis_size(name) + lax.axis_index(name)
        count = count * lax.axis_size(name)
    return index, count


def normalize(values, axis):
    centre = jnp.mean(values, axis=axis, keepdims=True)
    shifted = values - centre
    spread = jnp.mean(shifted * shifted, axis=axis, keepdims=True)
    return shifted * lax.rsqrt(spread + EPSILON)


def project_kernel(pair_ref, wz_ref, atom_ref, meta_ref, out_ref):
    rows, width = pair_ref.shape
    atoms = atom_ref.shape[0]
    channels = wz_ref.shape[1]
    eye = iota((width, width), 0) == iota((width, width), 1)
    centring = (eye.astype(F32) - 1.0 / width).astype(BF16)
    average = jnp.full((channels, width), 1.0 / width, BF16)
    wz_t = jnp.transpose(wz_ref[...].astype(F32)).astype(BF16)
    step = 512
    for first in range(0, rows, step):
        shifted = dot(pair_ref[first : first + step, :], centring)
        spread = dot_nt(average, (shifted * shifted).astype(BF16))
        projected = dot_nt(wz_t, shifted.astype(BF16))
        projected = (projected * lax.rsqrt(spread + EPSILON)).astype(BF16)
        for part in range(step // LANES):
            row = atoms + channels * ((first // LANES) + part)
            out_ref[row : row + channels, :] = projected[:, LANES * part : LANES * (part + 1)]
    out_ref[0:atoms, :] = atom_ref[...]
    row = atoms + channels * (rows // LANES)
    out_ref[row : row + 16, :] = meta_ref[...]


def spread_weight(weight_t, rows, ratio):
    side = weight_t.shape[1]
    cols = 256
    right = (iota((cols, side), 0) % side == iota((cols, side), 1)).astype(BF16)
    full = dot_nt(weight_t, right)
    same = (iota((rows, cols), 0) % ratio) == (iota((rows, cols), 1) // side)
    return jnp.where(same, full, 0.0).astype(BF16)


def main_kernel(
    own_ref,
    left_ref,
    right_ref,
    w_single_ref,
    w_mlp_ref,
    w_bias_ref,
    w_attn_ref,
    w_out_ref,
    w_in_ref,
    w_trans_out_ref,
    w_token_ref,
    token_out_ref,
    atom_out_ref,
    scalars_vmem,
    scalars,
    token_rows,
    key_terms,
    query_terms,
    tables,
    bias_ref,
    act_ref,
    query_ref,
    gate_ref,
    key_ref,
    value_ref,
    gated_ref,
    feature_ref,
    sem,
):
    index, count = shard_place()
    atoms, width = atom_out_ref.shape
    tokens = token_out_ref.shape[0]
    channels = w_mlp_ref.shape[1]
    heads = w_bias_ref.shape[2]
    head_size = width // heads
    tiles = atoms // LANES
    pairs = tokens // 2
    meta = atoms + channels * pairs
    first_valid = jnp.where(index == 0, atoms, 0)
    end_valid = jnp.where(index == count - 1, 2 * atoms, 3 * atoms)

    sides = (left_ref, own_ref, right_ref)
    shift_of = (-tokens, 0, tokens)
    number = iota((3 * tiles, LANES), 0) * LANES + iota((3 * tiles, LANES), 1)
    relative = jnp.concatenate(
        [ref[meta : meta + 16, :].astype(F32)[0:tiles] + s for ref, s in zip(sides, shift_of)],
        axis=0,
    )
    inside = (number >= first_valid) & (number < end_valid)
    relative = jnp.where(inside, relative, -64.0)
    relative_int = relative.astype(jnp.int32)
    metas = [ref[meta : meta + 16, :].astype(F32) for ref in sides]
    offset_lanes = atoms // QB
    offset_row = (
        metas[0][3:4]
        + pltpu.roll(metas[1][3:4], offset_lanes, 1)
        + pltpu.roll(metas[2][3:4], 2 * offset_lanes, 1)
    )
    scalars_vmem[0 : 3 * tiles, :] = jnp.clip(relative_int, 0, 3 * tokens - 1)
    scalars_vmem[3 * tiles : 3 * tiles + 1, :] = offset_row.astype(jnp.int32)
    copy = pltpu.make_async_copy(scalars_vmem, scalars, sem)
    copy.start()
    for tile in range(3 * tiles):
        token_rows[tile] = jnp.broadcast_to(relative_int[tile : tile + 1], (8, LANES))
    token_rows[3 * tiles] = jnp.zeros((8, LANES), jnp.int32)

    w_query_t = jnp.transpose(w_single_ref[0].astype(F32)).astype(BF16)
    w_key_t = jnp.transpose(w_single_ref[1].astype(F32)).astype(BF16)
    w_terms = jnp.concatenate([w_query_t, w_key_t], axis=0)
    for side, ref in enumerate(sides):
        for tile in range(tiles):
            rows = ref[tile * LANES : (tile + 1) * LANES, :]
            at = side * tiles + tile
            act_ref[at * LANES : (at + 1) * LANES, :] = rows.astype(F32)
            terms = dot_nt(w_terms, jnp.maximum(rows, jnp.zeros((), BF16)))
            query_terms[at] = terms[0:channels]
            key_terms[at] = terms[channels:].astype(BF16).astype(F32)
        for pair in range(pairs):
            row = atoms + channels * pair
            tables[side * pairs + pair] = ref[row : row + channels, :].astype(F32)
    key_terms[3 * tiles] = jnp.zeros((channels, LANES), F32)

    big = 256
    group = big // channels
    select = (iota((big, channels), 0) % channels == iota((big, channels), 1)).astype(BF16)
    same_block = (iota((big, big), 0) // channels) == (iota((big, big), 1) // channels)
    mlp = []
    for layer in range(3):
        by_row = dot_nt(select, w_mlp_ref[layer]).astype(BF16)
        mlp.append(jnp.where(same_block, dot_nt(by_row, select), 0.0).astype(BF16))
    per_block = heads * group
    pick_head = (iota((per_block, heads), 0) // group == iota((per_block, heads), 1)).astype(BF16)
    same_query = (iota((per_block, big), 0) % group) == (iota((per_block, big), 1) // channels)
    bias_parts = []
    for layer in range(BLOCKS):
        by_row = dot_nt(pick_head, w_bias_ref[layer]).astype(BF16)
        bias_parts.append(jnp.where(same_query, dot_nt(by_row, select), 0.0).astype(BF16))
    bias_weight = jnp.concatenate(bias_parts, axis=0)

    copy.wait()
    lane = iota((channels, LANES), 1)
    lane8 = iota((8, LANES), 1)
    first_query = 2 * HALO
    window_count = (atoms + HALO + 4 * HALO) // QB

    def key_start(n):
        return HALO + QB * n + scalars[3 * tiles, n + offset_lanes - 2 * HALO // QB]

    def bias_window(n, carry):
        query = first_query + QB * n
        query_tile = query // LANES
        query_lane = query % LANES
        start = key_start(n)
        tile = start // LANES
        shift = start % LANES
        back = LANES - shift
        key_tokens = pltpu.roll(
            jnp.where(lane8 >= shift, token_rows[tile], token_rows[tile + 1]), back, 1
        )
        key_side = pltpu.roll(
            jnp.where(lane >= shift, key_terms[tile], key_terms[tile + 1]), back, 1
        )
        query_side = pltpu.roll(query_terms[query_tile], LANES - query_lane, 1)
        pieces = []
        for i in range(QB):
            token = scalars[query_tile, query_lane + i]
            low = (token & 1) * (LANES // 2)
            column = jnp.clip(
                key_tokens + (low + LANES // 4 - token), low, low + LANES // 2 - 1
            )
            table = tables[token >> 1]
            gathered = [
                jnp.take_along_axis(
                    table[8 * g : 8 * (g + 1)], column, axis=1, mode="promise_in_bounds"
                )
                for g in range(channels // 8)
            ]
            pieces.append(
                jnp.concatenate(gathered, axis=0) + key_side + query_side[:, i : i + 1]
            )
        half = QB // 2
        start_pair = jnp.concatenate(
            [jnp.concatenate(pieces[:half], axis=0), jnp.concatenate(pieces[half:], axis=0)],
            axis=1,
        )
        hidden = start_pair
        for layer in range(3):
            hidden = dot(mlp[layer], jnp.maximum(hidden, 0.0).astype(BF16))
        pair = (start_pair + hidden).reshape(group, channels, big)
        normed = normalize(pair, 1).reshape(big, big).astype(BF16)
        bias = dot(bias_weight, normed)
        for layer in range(BLOCKS):
            part = bias[layer * per_block : (layer + 1) * per_block]
            bias_ref[n, layer, 0:per_block, :] = part[:, 0:LANES]
            bias_ref[n, layer, per_block : 2 * per_block, :] = part[:, LANES:]
        return carry

    lax.fori_loop(0, window_count, bias_window, 0)

    head_of_lane = iota((QB // 2, width), 1) // head_size
    scale = 1.0 / math.sqrt(head_size)

    def project(layer, first, rows, chunk):
        for row in range(first, first + rows, chunk):
            where = slice(row, row + chunk)
            normed = normalize(act_ref[where, :], 1).astype(BF16)
            number = iota((chunk, width), 0) + row
            held = (number >= first_valid) & (number < end_valid)
            query_ref[where, :] = dot(normed, w_attn_ref[layer, 0]) * scale
            key_ref[where, :] = jnp.where(held, dot(normed, w_attn_ref[layer, 1]), 0.0)
            value_ref[where, :] = jnp.where(held, dot(normed, w_attn_ref[layer, 2]), 0.0)
            gate_ref[where, :] = dot(normed, w_attn_ref[layer, 3])

    def attend(layer, n):
        query = pl.multiple_of(first_query + QB * n, QB)
        start = key_start(n)
        q = query_ref[pl.ds(query, QB), :]
        k = key_ref[pl.ds(start, KW), :].astype(BF16)
        v = value_ref[pl.ds(start, KW), :].astype(BF16)
        number = iota((KW, LANES), 0) + start
        held = jnp.where((number >= first_valid) & (number < end_valid), 1.0, 0.0).astype(BF16)
        blocks = []
        for half in range(2):
            part = q[half * QB // 2 : (half + 1) * QB // 2]
            for h in range(heads):
                blocks.append(jnp.where(head_of_lane == h, part, 0.0).astype(BF16))
        scores = dot_nt(jnp.concatenate(blocks, axis=0), k) + bias_ref[n, layer]
        weights = jnp.exp(scores).astype(BF16)
        sums = dot(weights, jnp.concatenate([v, held], axis=1))
        halves = []
        for half in range(2):
            base = half * per_block
            total = sums[base : base + group]
            for h in range(1, heads):
                row = base + h * group
                chosen = jnp.concatenate([head_of_lane == h] * 2, axis=1)
                total = jnp.where(chosen, sums[row : row + group], total)
            halves.append(total[:, :LANES] / total[:, LANES:])
        attended = jnp.concatenate(halves, axis=0)
        gated_ref[pl.ds(query, QB), :] = attended * jax.nn.sigmoid(
            gate_ref[pl.ds(query, QB), :]
        )

    def dense(layer, first, rows, chunk):
        for row in range(first, first + rows, chunk):
            where = slice(row, row + chunk)
            number = iota((chunk, width), 0) + row
            held = (number >= first_valid) & (number < end_valid)
            act = act_ref[where, :] + dot(gated_ref[where, :].astype(BF16), w_out_ref[layer])
            act = jnp.where(held, act, 0.0)
            normed = normalize(act, 1).astype(BF16)
            gate_part = dot(normed, w_in_ref[layer, 0])
            up_part = dot(normed, w_in_ref[layer, 1])
            hidden = (gate_part / (1.0 + jnp.exp(-gate_part)) * up_part).astype(BF16)
            act_ref[where, :] = act + dot(hidden, w_trans_out_ref[layer])

    chunk_of = (288, 336, 240)
    for layer in range(BLOCKS):
        first_window = layer * HALO // QB
        last_window = window_count - layer * HALO // QB
        query_first = first_query + QB * first_window
        query_rows = QB * (last_window - first_window)
        key_first = query_first - HALO
        key_rows = query_rows + 2 * HALO
        project(layer, key_first, key_rows, key_rows // 3)

        def attend_step(step, carry):
            for w in range(CHUNK):
                attend(layer, first_window + step * CHUNK + w)
            return carry

        lax.fori_loop(0, (last_window - first_window) // CHUNK, attend_step, 0)
        dense(layer, query_first, query_rows, chunk_of[layer])

    atom_out_ref[...] = act_ref[atoms : 2 * atoms, :].astype(BF16)
    reach = atoms + LANES
    feature_ref[atoms + HALO : reach, :] = jnp.zeros_like(feature_ref[atoms + HALO : reach, :])
    for row in range(0, atoms + HALO, 160):
        rows = act_ref[atoms + row : atoms + row + 160, :].astype(BF16)
        features = jnp.maximum(dot(rows, w_token_ref[...]), 0.0)
        feature_ref[row : row + 160, :] = features.astype(BF16)
    slot = iota((tokens, LANES), 0) + tokens
    member = jnp.concatenate(
        [
            (slot == relative_int[tile : tile + 1]).astype(F32)
            for tile in range(tiles, 2 * tiles + 1)
        ],
        axis=1,
    ).astype(BF16)
    sums = dot(member, feature_ref[...])
    diagonal = (iota((tokens, LANES), 0) == iota((tokens, LANES), 1)).astype(F32)
    atoms_of = jnp.sum(diagonal * metas[1][4:5], axis=1, keepdims=True)
    token_out_ref[...] = (sums / atoms_of).astype(BF16)


def shards(
    atom_single,
    atom_token,
    token_atoms,
    window_offset,
    token_pair,
    w_zpair,
    w_single,
    w_pair_mlp,
    w_bias,
    w_attn,
    w_out,
    w_trans_in,
    w_trans_out,
    w_token,
):
    index, count = shard_place()
    atoms, width = atom_single.shape
    tokens, band, depth = token_pair.shape
    channels = w_zpair.shape[1]
    tiles = atoms // LANES
    pairs = tokens * band // LANES
    payload_rows = atoms + channels * pairs + 16

    local = (atom_token - (index - 1) * tokens).reshape(tiles, LANES)
    meta = jnp.concatenate(
        [
            local,
            jnp.pad(window_offset, (0, LANES - window_offset.shape[0]))[None],
            jnp.pad(token_atoms, (0, LANES - tokens))[None],
            jnp.zeros((16 - tiles - 2, LANES), jnp.int32),
        ],
        axis=0,
    ).astype(BF16)
    vmem = pl.BlockSpec(memory_space=pltpu.VMEM)
    payload = pl.pallas_call(
        project_kernel,
        out_shape=jax.ShapeDtypeStruct((payload_rows, width), BF16),
        in_specs=[vmem] * 4,
        out_specs=vmem,
        name="project",
    )(token_pair.reshape(tokens * band, depth), w_zpair, atom_single, meta)
    up = [(i, i + 1) for i in range(count - 1)]
    down = [(i + 1, i) for i in range(count - 1)]
    left = lax.ppermute(payload, RING, up)
    right = lax.ppermute(payload, RING, down)

    reach = 3 * atoms
    windows = (atoms + 5 * HALO) // QB
    heads = w_bias.shape[2]
    channels_out = w_token.shape[1]
    token_single, atom_out = pl.pallas_call(
        main_kernel,
        out_shape=(
            jax.ShapeDtypeStruct((tokens, channels_out), BF16),
            jax.ShapeDtypeStruct((atoms, width), BF16),
        ),
        in_specs=[vmem] * 11,
        out_specs=(vmem, vmem),
        scratch_shapes=[
            pltpu.VMEM((16, LANES), jnp.int32),
            pltpu.SMEM((16, LANES), jnp.int32),
            pltpu.VMEM((3 * tiles + 1, 8, LANES), jnp.int32),
            pltpu.VMEM((3 * tiles + 1, channels, LANES), F32),
            pltpu.VMEM((3 * tiles, channels, LANES), F32),
            pltpu.VMEM((3 * pairs, channels, LANES), F32),
            pltpu.VMEM((windows, BLOCKS, heads * QB, KW), F32),
            pltpu.VMEM((reach, width), F32),
            pltpu.VMEM((reach, width), F32),
            pltpu.VMEM((reach, width), F32),
            pltpu.VMEM((reach, width), F32),
            pltpu.VMEM((reach, width), F32),
            pltpu.VMEM((reach, width), F32),
            pltpu.VMEM((atoms + LANES, channels_out), BF16),
            pltpu.SemaphoreType.DMA,
        ],
        compiler_params=pltpu.CompilerParams(vmem_limit_bytes=48 * 2**20),
        name="encode",
    )(
        payload,
        left,
        right,
        w_single,
        w_pair_mlp,
        w_bias,
        w_attn,
        w_out,
        w_trans_in,
        w_trans_out,
        w_token,
    )
    return token_single, atom_out


def solution(mesh):
    split = ("group", "seq", "chan", "sub")
    in_specs = (
        P(split, None),
        P(split),
        P(split),
        P(split),
        P(split, None, None),
        P(),
        P(),
        P(),
        P(),
        P(),
        P(),
        P(),
        P(),
        P(),
    )
    out_specs = (P(split, None), P(split, None))
    return jax.shard_map(shards, mesh=mesh, in_specs=in_specs, out_specs=out_specs, check_vma=False)
```

time: 305 us -> 73 us (0.24)
  local copies, waits for them, and re-layouts: 222 us -> 3.3 us
  Pallas kernels: 0 us -> 56.7 us
  matrix products: 30 us -> 0 us
  starting transfers between devices: 26.5 us -> 6.42 us
  other arithmetic: 11.8 us -> 2.02 us
  waiting for transfers between devices: 10.6 us -> 3.17 us
    gather x6 -> x0, local copies, waits for them, and re-layouts: 201 us -> none  [the longest x2 181 us: shards(): jnp.take(flat_band, flat_index.reshape(-1), axis=1)]
    pallas_call x0 -> x2, Pallas kernels: none -> 56.7 us  [the longest x1 53.3 us: shards(): pl.pallas_call(main_kernel, out_shape=(jax.ShapeDtypeStruct((tokens, chan...]
    dot_general x24 -> x0, matrix products: 24.5 us -> none  [the longest x1 3.52 us: pair_bias(): jnp.einsum('enqk,ef->fnqk', jax.nn.relu(pair_start), mlp_f[0], precision=...]
    ppermute x10 -> x2, starting transfers between devices: 26.5 us -> 6.42 us  [the longest x1 4.46 us: shards(): left = lax.ppermute(payload, RING, up)]
    unnamed x76 -> x23, local copies, waits for them, and re-layouts: 11.3 us -> 3.22 us
    ppermute x10 -> x2, waiting for transfers between devices: 10.6 us -> 3.17 us  [the longest x1 2.42 us: shards(): left = lax.ppermute(payload, RING, up)]
    div x3 -> x0, matrix products: 5.49 us -> none  [shards(): weights / jnp.sum(weights, axis=3, keepdims=True)]
    reduce_sum x10 -> x0, other arithmetic: 4.23 us -> none  [the longest x8 3.31 us: normalize(): spread = jnp.mean(shifted * shifted, axis=axis, keepdims=True)]
  transfers between devices with their start and end apart: 10 -> 2, of which waited for: 3 -> 2; matrix products, arithmetic and copies ran while one was open for 7% -> 1% of each run, Pallas kernels for 0% -> 0%
where the time goes in v1:
time: 73 us; the launch traced here: 72.3 us
  Pallas kernels  56.7 us (78%)
  starting transfers between devices  6.42 us (9%)
  local copies, waits for them, and re-layouts  3.3 us (5%)
  waiting for transfers between devices  3.17 us (4%)
  other arithmetic  2.02 us (3%)
  between operations  0.74 us (1%)
    pallas_call x1, Pallas kernels, shards(): pl.pallas_call(main_kernel, out_shape=(jax.ShapeDtypeStruct((tokens, chan...  53.3 us
    ppermute x1, starting transfers between devices, shards(): left = lax.ppermute(payload, RING, up)  4.46 us
    pallas_call x1, Pallas kernels, shards(): pl.pallas_call(project_kernel, out_shape=jax.ShapeDtypeStruct((payload_ro...  3.39 us
    unnamed x23, local copies, waits for them, and re-layouts  3.22 us
    ppermute x1, waiting for transfers between devices, shards(): left = lax.ppermute(payload, RING, up)  2.42 us
    ppermute x1, starting transfers between devices, shards(): right = lax.ppermute(payload, RING, down)  1.95 us
  transfers between devices with their start and end apart: 2, of which 2 were waited for; matrix products, arithmetic and copies ran while one was open for 1% of the time, Pallas kernels for 0%

profile of v1, /device:TPU:1, one launch (start us, length us, event | category | flops | bytes accessed | tf_op | source)
XLA Modules:
  0.0 72.3 jit_solution(12165653826503462822)
XLA Ops:
  0.6 0.0 copy-start.6
  0.6 0.0 copy-start.9
  0.7 0.0 copy-start.8
  0.7 0.0 copy-start.5
  0.7 0.6 copy-done.9
  1.3 0.7 convert.19
  2.0 0.0 copy-done.8
  2.0 0.7 copy.16.wz_ref
  2.7 0.7 fusion
  3.4 0.1 pad.15.clone
  3.5 0.7 maximum_maximum_fusion.meta_ref
  4.1 0.0 copy-start.7
  4.1 0.0 copy-start.1
  4.1 0.0 copy-start.2
  4.1 0.0 copy-start.4
  4.2 3.4 %project.1.own_ref = bf16[784,128]{1,0:T(8,128)(2,1)} custom-call(bf16[3072,128]{1,0:T(8,128)(2,1)} %bitcast.7, bf16[128,16]{1,0:T(8,128)(2,1)} %copy.16.wz_ref, bf16[384,128]{1,0:T(8,128)(2,1)} %atom_ref.1, bf16[16,128]{1,0:T(8,128)(2,1)} %maximum_maximum_fusion.meta_ref), custom_call_target="tpu_custom_call" | custom-call | tf_op jit(solution)/shard_map/project/pallas_call | solution.py:373
  7.5 2.0 %collective-permute-start.1 = (bf16[784,128]{1,0:T(8,128)(2,1)}, bf16[784,128]{1,0:T(8,128)(2,1)S(1)}, u32[]{:S(2)}, u32[]{:S(2)}) collective-permute-start(bf16[784,128]{1,0:T(8,128)(2,1)} %project.1.own_ref), channel_id=1, source_target_pairs={{1,0},{2,1},{3,2},{4,3},{5,4},{6,5},{7,6},{8,7},{9,8},{10,9},{11,1... | collective-permute-start | bytes 602120 | tf_op jit(solution)/shard_map/ppermute | solution.py:383
  9.5 4.5 %collective-permute-start = (bf16[784,128]{1,0:T(8,128)(2,1)}, bf16[784,128]{1,0:T(8,128)(2,1)S(1)}, u32[]{:S(2)}, u32[]{:S(2)}) collective-permute-start(bf16[784,128]{1,0:T(8,128)(2,1)} %project.1.own_ref), channel_id=1, source_target_pairs={{0,1},{1,2},{2,3},{3,4},{4,5},{5,6},{6,7},{7,8},{8,9},{9,10},{10,1... | collective-permute-start | bytes 602120 | tf_op jit(solution)/shard_map/ppermute | solution.py:382
  14.0 0.8 %copy.18.w_bias_ref = bf16[3,16,4]{2,1,0:T(8,128)(2,1)S(1)} copy(bf16[3,16,4]{1,2,0:T(4,128)(2,1)} %param.22) | data formatting | bytes 768 | tf_op args[8]
  14.8 0.0 copy-done.7
  14.8 0.1 copy.17.w_single_ref
  14.9 0.7 %collective-permute-done.1.right_ref = bf16[784,128]{1,0:T(8,128)(2,1)S(1)} collective-permute-done((bf16[784,128]{1,0:T(8,128)(2,1)}, bf16[784,128]{1,0:T(8,128)(2,1)S(1)}, u32[]{:S(2)}, u32[]{:S(2)}) %collective-permute-start.1) | collective-permute-done | bytes 200736 | tf_op jit(solution)/shard_map/ppermute | solution.py:383
  15.6 2.4 %collective-permute-done.left_ref = bf16[784,128]{1,0:T(8,128)(2,1)S(1)} collective-permute-done((bf16[784,128]{1,0:T(8,128)(2,1)}, bf16[784,128]{1,0:T(8,128)(2,1)S(1)}, u32[]{:S(2)}, u32[]{:S(2)}) %collective-permute-start) | collective-permute-done | bytes 200736 | tf_op jit(solution)/shard_map/ppermute | solution.py:382
  18.1 0.0 copy-done.6
  18.1 0.0 copy-done.5
  18.1 0.0 copy-done.1
  18.1 0.0 copy-done.2
  18.1 0.0 copy-done.3
  18.1 0.0 copy-done.4
  18.1 0.0 copy-start
  18.1 0.9 %copy-done = bf16[784,128]{1,0:T(8,128)(2,1)S(1)} copy-done((bf16[784,128]{1,0:T(8,128)(2,1)S(1)}, bf16[784,128]{1,0:T(8,128)(2,1)}, u32[]{:S(2)}) %copy-start) | copy-done | bytes 200728
  19.0 53.3 %encode.1 = (bf16[48,768]{1,0:T(8,128)(2,1)}, bf16[384,128]{1,0:T(8,128)(2,1)}) custom-call(bf16[784,128]{1,0:T(8,128)(2,1)S(1)} %copy-done, bf16[784,128]{1,0:T(8,128)(2,1)S(1)} %collective-permute-done.left_ref, bf16[784,128]{1,0:T(8,128)(2,1)S(1)} %collective-permute-done.1.right_ref, bf16[2,128,16]{2,1,0:T(8,128)(2,1)S(1)} %copy.17.w_single_ref, ...), custom_call_target="tpu_custom_call" | custom-call | tf_op jit(solution)/shard_map/encode/pallas_call | solution.py:389
  (4 shorter events, 0.0 us)
Async XLA Ops:
  0.6 17.4 %copy-start.6 = (bf16[3,16,16]{2,1,0:T(8,128)(2,1)S(1)}, bf16[3,16,16]{2,1,0:T(8,128)(2,1)}, u32[]{:S(2)}) copy-start(bf16[3,16,16]{2,1,0:T(8,128)(2,1)} %w_mlp_ref.1) | copy-start | bytes 4612
  0.6 0.7 copy-start.9
  0.7 1.3 %copy-start.8 = (bf16[128,16]{0,1:T(8,128)(2,1)S(1)}, bf16[128,16]{0,1:T(8,128)(2,1)}, u32[]{:S(2)}) copy-start(bf16[128,16]{0,1:T(8,128)(2,1)} %param.19) | copy-start | bytes 12292
  0.7 17.4 %copy-start.5 = (bf16[3,128,128]{2,1,0:T(8,128)(2,1)S(1)}, bf16[3,128,128]{2,1,0:T(8,128)(2,1)}, u32[]{:S(2)}) copy-start(bf16[3,128,128]{2,1,0:T(8,128)(2,1)} %w_out_ref.1) | copy-start | bytes 294916
  4.1 10.6 %copy-start.7 = (bf16[2,128,16]{1,2,0:T(8,128)(2,1)S(1)}, bf16[2,128,16]{1,2,0:T(8,128)(2,1)}, u32[]{:S(2)}) copy-start(bf16[2,128,16]{1,2,0:T(8,128)(2,1)} %param.20) | copy-start | bytes 24580
  4.1 13.9 %copy-start.1 = (bf16[3,4,128,128]{3,2,1,0:T(8,128)(2,1)S(1)}, bf16[3,4,128,128]{3,2,1,0:T(8,128)(2,1)}, u32[]{:S(2)}) copy-start(bf16[3,4,128,128]{3,2,1,0:T(8,128)(2,1)} %w_attn_ref.1) | copy-start | bytes 1179652
  4.1 13.9 %copy-start.2 = (bf16[3,2,128,256]{3,2,1,0:T(8,128)(2,1)S(1)}, bf16[3,2,128,256]{3,2,1,0:T(8,128)(2,1)}, u32[]{:S(2)}) copy-start(bf16[3,2,128,256]{3,2,1,0:T(8,128)(2,1)} %w_in_ref.1) | copy-start | bytes 1179652
  4.1 13.9 %copy-start.3 = (bf16[3,256,128]{2,1,0:T(8,128)(2,1)S(1)}, bf16[3,256,128]{2,1,0:T(8,128)(2,1)}, u32[]{:S(2)}) copy-start(bf16[3,256,128]{2,1,0:T(8,128)(2,1)} %w_trans_out_ref.1) | copy-start | bytes 589828
  4.1 13.9 %copy-start.4 = (bf16[128,768]{1,0:T(8,128)(2,1)S(1)}, bf16[128,768]{1,0:T(8,128)(2,1)}, u32[]{:S(2)}) copy-start(bf16[128,768]{1,0:T(8,128)(2,1)} %w_token_ref.1) | copy-start | bytes 589828
  7.5 8.1 %collective-permute-start.1 = (bf16[784,128]{1,0:T(8,128)(2,1)}, bf16[784,128]{1,0:T(8,128)(2,1)S(1)}, u32[]{:S(2)}, u32[]{:S(2)}) collective-permute-start(bf16[784,128]{1,0:T(8,128)(2,1)} %project.1.own_ref), channel_id=1, source_target_pairs={{1,0},{2,1},{3,2},{4,3},{5,4},{6,5},{7,6},{8,7},{9,8},{10,9},{11,1... | collective-permute-start | bytes 602120 | tf_op jit(solution)/shard_map/ppermute | solution.py:383
  9.5 8.6 %collective-permute-start = (bf16[784,128]{1,0:T(8,128)(2,1)}, bf16[784,128]{1,0:T(8,128)(2,1)S(1)}, u32[]{:S(2)}, u32[]{:S(2)}) collective-permute-start(bf16[784,128]{1,0:T(8,128)(2,1)} %project.1.own_ref), channel_id=1, source_target_pairs={{0,1},{1,2},{2,3},{3,4},{4,5},{5,6},{6,7},{7,8},{8,9},{9,10},{10,1... | collective-permute-start | bytes 602120 | tf_op jit(solution)/shard_map/ppermute | solution.py:382
  18.1 0.9 %copy-start = (bf16[784,128]{1,0:T(8,128)(2,1)S(1)}, bf16[784,128]{1,0:T(8,128)(2,1)}, u32[]{:S(2)}) copy-start(bf16[784,128]{1,0:T(8,128)(2,1)} %project.1.own_ref) | copy-start | bytes 602116

commit v2 on v1

v2 whole, which is shorter than its diff:
```python
import math

import jax
import jax.numpy as jnp
from jax import lax
from jax.experimental import pallas as pl
from jax.experimental.pallas import tpu as pltpu
from jax.sharding import PartitionSpec as P

BLOCKS = 3
QB = 32
KW = 128
HALO = 96
LANES = 128
PAIR_DEPTH = 6
PAIR_SLOTS = 4
PAIR_UNROLL = 3
EPSILON = 1e-05
RING = ("seq", "chan", "sub")
NT = (((1,), (1,)), ((), ()))
F32 = jnp.float32
BF16 = jnp.bfloat16


def dot(a, b):
    return jnp.dot(a, b, preferred_element_type=F32)


def dot_nt(a, b):
    return lax.dot_general(a, b, NT, preferred_element_type=F32)


def iota(shape, axis):
    return lax.broadcasted_iota(jnp.int32, shape, axis)


def shard_place():
    index, count = 0, 1
    for name in RING:
        index = index * lax.axis_size(name) + lax.axis_index(name)
        count = count * lax.axis_size(name)
    return index, count


def normalize(values, axis):
    centre = jnp.mean(values, axis=axis, keepdims=True)
    shifted = values - centre
    spread = jnp.mean(shifted * shifted, axis=axis, keepdims=True)
    return shifted * lax.rsqrt(spread + EPSILON)


def project_kernel(pair_ref, wz_ref, atom_ref, meta_ref, out_ref):
    rows, width = pair_ref.shape
    atoms = atom_ref.shape[0]
    channels = wz_ref.shape[0]
    eye = iota((width, width), 0) == iota((width, width), 1)
    centring = (eye.astype(F32) - 1.0 / width).astype(BF16)
    average = jnp.full((channels, width), 1.0 / width, BF16)
    step = 512
    for first in range(0, rows, step):
        shifted = dot(pair_ref[first : first + step, :], centring)
        spread = dot_nt(average, (shifted * shifted).astype(BF16))
        projected = dot_nt(wz_ref[...], shifted.astype(BF16))
        projected = (projected * lax.rsqrt(spread + EPSILON)).astype(BF16)
        for part in range(step // LANES):
            row = atoms + channels * ((first // LANES) + part)
            out_ref[row : row + channels, :] = projected[:, LANES * part : LANES * (part + 1)]
    out_ref[0:atoms, :] = atom_ref[...]
    row = atoms + channels * (rows // LANES)
    out_ref[row : row + 16, :] = meta_ref[...]


def main_kernel(
    own_ref,
    left_ref,
    right_ref,
    w_single_ref,
    w_mlp_ref,
    w_bias_ref,
    w_attn_ref,
    w_out_ref,
    w_in_ref,
    w_trans_out_ref,
    w_token_ref,
    token_out_ref,
    atom_out_ref,
    scalars_vmem,
    scalars,
    token_rows,
    key_terms,
    token_shift,
    token_base,
    table_rows,
    band_ref,
    side_ref,
    column_ref,
    start_ref,
    pair_ref,
    first_ref,
    second_ref,
    third_ref,
    normed_ref,
    left_terms,
    right_terms,
    mlp_ref,
    bias_weight_ref,
    bias_ref,
    act_ref,
    held_ref,
    query_ref,
    gate_ref,
    key_ref,
    value_ref,
    gated_ref,
    feature_ref,
    sem,
):
    index, count = shard_place()
    atoms, width = atom_out_ref.shape
    tokens = token_out_ref.shape[0]
    channels = w_mlp_ref.shape[1]
    heads = w_bias_ref.shape[1]
    head_size = width // heads
    tiles = atoms // LANES
    pairs = tokens // 2
    meta = atoms + channels * pairs
    first_valid = jnp.where(index == 0, atoms, 0)
    end_valid = jnp.where(index == count - 1, 2 * atoms, 3 * atoms)
    first_query = 2 * HALO
    window_count = (atoms + HALO + 4 * HALO) // QB
    query_end = first_query + QB * window_count

    sides = (left_ref, own_ref, right_ref)
    metas = [ref[meta : meta + 16, :].astype(F32) for ref in sides]
    number = iota((3 * tiles, LANES), 0) * LANES + iota((3 * tiles, LANES), 1)
    relative = jnp.concatenate(
        [m[0:tiles] + s for m, s in zip(metas, (-tokens, 0, tokens))], axis=0
    )
    inside = (number >= first_valid) & (number < end_valid)
    relative = jnp.where(inside, relative, -64.0)
    relative_int = relative.astype(jnp.int32)
    offset_lanes = atoms // QB
    offset_row = (
        metas[0][3:4]
        + pltpu.roll(metas[1][3:4], offset_lanes, 1)
        + pltpu.roll(metas[2][3:4], 2 * offset_lanes, 1)
    )
    scalars_vmem[...] = jnp.broadcast_to(offset_row, (8, LANES)).astype(jnp.int32)
    copy = pltpu.make_async_copy(scalars_vmem, scalars, sem)
    copy.start()
    for tile in range(3 * tiles):
        token_rows[tile] = jnp.broadcast_to(relative_int[tile : tile + 1], (8, LANES))
    token_rows[3 * tiles] = jnp.zeros((8, LANES), jnp.int32)

    big = 256
    group = big // channels
    select = (iota((big, channels), 0) // group == iota((big, channels), 1)).astype(BF16)
    same_query = (iota((big, big), 0) % group) == (iota((big, big), 1) % group)
    for layer in range(3):
        by_row = dot_nt(select, w_mlp_ref[layer]).astype(BF16)
        mlp_ref[layer] = jnp.where(same_query, dot_nt(by_row, select), 0.0).astype(BF16)
    per_block = heads * group
    pick_head = (iota((per_block, heads), 0) // group == iota((per_block, heads), 1)).astype(BF16)
    for layer in range(BLOCKS):
        by_row = dot(pick_head, w_bias_ref[layer]).astype(BF16)
        bias_weight_ref[layer * per_block : (layer + 1) * per_block, :] = jnp.where(
            same_query[0:per_block], dot_nt(by_row, select), 0.0
        ).astype(BF16)

    eye = iota((LANES, LANES), 0) == iota((LANES, LANES), 1)
    ones = jnp.ones((LANES, LANES), BF16)
    for side, ref in enumerate(sides):
        for tile in range(tiles):
            rows = ref[tile * LANES : (tile + 1) * LANES, :]
            at = side * tiles + tile
            where = slice(at * LANES, (at + 1) * LANES)
            act_ref[where, :] = rows.astype(F32)
            held_ref[where, :] = (
                (iota((LANES, LANES), 0) + at * LANES >= first_valid)
                & (iota((LANES, LANES), 0) + at * LANES < end_valid)
            ).astype(F32)
            relu = jnp.maximum(rows, jnp.zeros((), BF16))
            key_terms[at] = dot_nt(w_single_ref[1], relu).astype(BF16).astype(F32)
            column = dot(jnp.where(eye, relative[at : at + 1], 0.0).astype(BF16), ones)
            column = column.astype(jnp.int32)
            base = (column & 1) * (LANES // 2)
            token_base[where, :] = base
            token_shift[where, :] = LANES // 4 - column
        for pair in range(pairs):
            row = atoms + channels * pair
            to = (side * pairs + pair) * channels
            table_rows[to : to + channels, :] = ref[row : row + channels, :].astype(F32)
    key_terms[3 * tiles] = jnp.zeros((channels, LANES), F32)

    w_query = jnp.transpose(w_single_ref[0].astype(F32))
    for tile in range(first_query // LANES, -(-query_end // LANES)):
        where = slice(tile * LANES, (tile + 1) * LANES)
        token = LANES // 4 - token_shift[where, :]
        hit = ((token >> 1) == iota((LANES, LANES), 1)).astype(F32).astype(BF16)
        left_terms[where, 0:LANES] = hit
        left_terms[where, LANES:] = jnp.maximum(act_ref[where, :], 0.0).astype(BF16)
    padded = -(-3 * pairs // 16) * 16
    for c in range(channels):
        at = slice(c % 2 * LANES, (c % 2 + 1) * LANES)
        rows = [
            table_rows[pl.ds(8 * channels * g + c, 8, stride=channels), :]
            for g in range(3 * pairs // 8)
        ]
        rows.append(jnp.zeros((padded - 3 * pairs, LANES), F32))
        right_terms[c // 2, 0:padded, at] = jnp.concatenate(rows, axis=0).astype(BF16)
        right_terms[c // 2, padded:LANES, at] = jnp.zeros((LANES - padded, LANES), BF16)
        right_terms[c // 2, LANES:, at] = jnp.broadcast_to(
            w_query[:, c : c + 1], (width, LANES)
        ).astype(BF16)

    def band_step(step, carry):
        for c in range(2):
            band = dot(left_terms[first_query:query_end, :], right_terms[2 * step + c])
            for d in range(2):
                at = slice(d * LANES, (d + 1) * LANES)
                band_ref[4 * step + 2 * c + d, first_query:query_end, :] = band[:, at]
        return carry

    lax.fori_loop(0, channels // 4, band_step, 0)

    copy.wait()
    lane = iota((channels, LANES), 1)
    lane8 = iota((8, LANES), 1)
    log2e = math.log2(math.e)

    def key_start(n):
        return HALO + QB * n + scalars[0, n + offset_lanes - 2 * HALO // QB]

    def window_of(step, behind):
        return jnp.clip(step - behind, 0, window_count - 1)

    def column_stage(step):
        n = window_of(step, 0)
        query = pl.multiple_of(first_query + QB * n, QB)
        start = key_start(n)
        tile = start // LANES
        shift = start % LANES
        back = LANES - shift
        key_tokens = pltpu.roll(
            jnp.where(lane8 >= shift, token_rows[tile], token_rows[tile + 1]), back, 1
        )
        side_ref[...] = pltpu.roll(
            jnp.where(lane >= shift, key_terms[tile], key_terms[tile + 1]), back, 1
        )
        for g in range(QB // 8):
            rows = pl.ds(query + 8 * g, 8)
            column_ref[8 * g : 8 * g + 8, :] = (
                jnp.clip(key_tokens + token_shift[rows, :], 0, LANES // 2 - 1)
                + token_base[rows, :]
            )

    def start_stage(step):
        query = pl.multiple_of(first_query + QB * window_of(step, 1), QB)
        slot = step % PAIR_SLOTS
        for half in range(2):
            at = slice(half * LANES, (half + 1) * LANES)
            pieces = [[] for _ in range(channels)]
            for g in range(half * group // 8, (half + 1) * group // 8):
                column = column_ref[8 * g : 8 * g + 8, :]
                rows = pl.ds(query + 8 * g, 8)
                for e in range(channels):
                    pieces[e].append(
                        jnp.take_along_axis(
                            band_ref[e, rows, :], column, axis=1, mode="promise_in_bounds"
                        )
                        + jnp.broadcast_to(side_ref[e : e + 1, :], (8, LANES))
                    )
            for e in range(channels):
                piece = jnp.concatenate(pieces[e], axis=0)
                start_ref[slot, e * group : (e + 1) * group, at] = piece
                first_ref[e * group : (e + 1) * group, at] = jnp.maximum(
                    piece.astype(BF16), jnp.zeros((), BF16)
                )

    def hidden_stage(layer, from_ref, to_ref):
        hidden = dot(mlp_ref[layer], from_ref[...]).astype(BF16)
        to_ref[...] = jnp.maximum(hidden, jnp.zeros((), BF16))

    def sum_stage(step):
        pair_ref[...] = start_ref[(step + 1) % PAIR_SLOTS] + dot(mlp_ref[2], third_ref[...])

    def norm_stage():
        for half in range(2):
            at = slice(half * LANES, (half + 1) * LANES)
            pair = pair_ref[:, at].reshape(channels, group, LANES)
            shifted = pair - jnp.mean(pair, axis=0, keepdims=True)
            spread = jnp.mean(shifted * shifted, axis=0, keepdims=True)
            normed = shifted * (lax.rsqrt(spread + EPSILON) * log2e)
            normed_ref[:, at] = normed.reshape(big, LANES).astype(BF16)

    def bias_stage(step):
        n = window_of(step, PAIR_DEPTH)
        bias = dot(bias_weight_ref[...], normed_ref[...])
        for layer in range(BLOCKS):
            part = bias[layer * per_block : (layer + 1) * per_block]
            bias_ref[n, layer, 0:per_block, :] = part[:, 0:LANES]
            bias_ref[n, layer, per_block : 2 * per_block, :] = part[:, LANES:]

    def pair_step(outer, carry):
        for inner in range(PAIR_UNROLL):
            step = outer * PAIR_UNROLL + inner
            bias_stage(step)
            norm_stage()
            sum_stage(step)
            hidden_stage(1, second_ref, third_ref)
            hidden_stage(0, first_ref, second_ref)
            start_stage(step)
            column_stage(step)
        return carry

    lax.fori_loop(0, -(-(window_count + PAIR_DEPTH) // PAIR_UNROLL), pair_step, 0)

    head_of_lane = iota((QB // 2, width), 1) // head_size
    scale = log2e / math.sqrt(head_size)

    def project(layer, first, rows, chunk):
        w_first = jnp.concatenate([w_attn_ref[layer, 0], w_attn_ref[layer, 1]], axis=1)
        w_second = jnp.concatenate([w_attn_ref[layer, 2], w_attn_ref[layer, 3]], axis=1)
        for row in range(first, first + rows, chunk):
            where = slice(row, row + chunk)
            normed = normalize(act_ref[where, :], 1).astype(BF16)
            held = held_ref[where, :] > 0.0
            both = dot(normed, w_first)
            query_ref[where, :] = (both[:, :width] * scale).astype(BF16)
            key_ref[where, :] = jnp.where(held, both[:, width:], 0.0)
            both = dot(normed, w_second)
            value_ref[where, :] = jnp.where(held, both[:, :width], 0.0)
            gate_ref[where, :] = jax.nn.sigmoid(both[:, width:])

    def attend(layer, n):
        query = pl.multiple_of(first_query + QB * n, QB)
        start = key_start(n)
        q = query_ref[pl.ds(query, QB), :]
        k = key_ref[pl.ds(start, KW), :].astype(BF16)
        v = jnp.concatenate(
            [value_ref[pl.ds(start, KW), :], held_ref[pl.ds(start, KW), :]], axis=1
        ).astype(BF16)
        blocks = []
        for half in range(2):
            part = q[half * QB // 2 : (half + 1) * QB // 2]
            for h in range(heads):
                blocks.append(jnp.where(head_of_lane == h, part, jnp.zeros((), BF16)))
        scores = dot_nt(jnp.concatenate(blocks, axis=0), k) + bias_ref[n, layer]
        sums = dot(jnp.exp2(scores).astype(BF16), v)
        halves = []
        for half in range(2):
            base = half * per_block
            value = sums[base : base + group, :LANES]
            total = sums[base : base + group, LANES:]
            for h in range(1, heads):
                row = base + h * group
                value = jnp.where(head_of_lane == h, sums[row : row + group, :LANES], value)
                total = jnp.where(head_of_lane == h, sums[row : row + group, LANES:], total)
            halves.append(value / total)
        attended = jnp.concatenate(halves, axis=0)
        gated_ref[pl.ds(query, QB), :] = (attended * gate_ref[pl.ds(query, QB), :]).astype(BF16)

    def dense(layer, first, rows, chunk):
        for row in range(first, first + rows, chunk):
            where = slice(row, row + chunk)
            act = act_ref[where, :] + dot(gated_ref[where, :], w_out_ref[layer])
            act = jnp.where(held_ref[where, :] > 0.0, act, 0.0)
            normed = normalize(act, 1).astype(BF16)
            gate_part = dot(normed, w_in_ref[layer, 0])
            up_part = dot(normed, w_in_ref[layer, 1])
            hidden = (gate_part / (1.0 + jnp.exp(-gate_part)) * up_part).astype(BF16)
            act_ref[where, :] = act + dot(hidden, w_trans_out_ref[layer])

    chunk_of = (288, 336, 240)
    for layer in range(BLOCKS):
        first_window = layer * HALO // QB
        last_window = window_count - layer * HALO // QB
        windows = last_window - first_window
        query_first = first_query + QB * first_window
        query_rows = QB * windows
        key_first = query_first - HALO
        key_rows = query_rows + 2 * HALO
        project(layer, key_first, key_rows, key_rows // 3)

        def attend_step(step, carry):
            for w in range(windows // 3):
                attend(layer, first_window + step * (windows // 3) + w)
            return carry

        lax.fori_loop(0, 3, attend_step, 0)
        dense(layer, query_first, query_rows, chunk_of[layer])

    atom_out_ref[...] = act_ref[atoms : 2 * atoms, :].astype(BF16)
    reach = atoms + LANES
    feature_ref[atoms + HALO : reach, :] = jnp.zeros_like(feature_ref[atoms + HALO : reach, :])
    for row in range(0, atoms + HALO, 160):
        rows = act_ref[atoms + row : atoms + row + 160, :].astype(BF16)
        features = jnp.maximum(dot(rows, w_token_ref[...]), 0.0)
        feature_ref[row : row + 160, :] = features.astype(BF16)
    slot = iota((tokens, LANES), 0) + tokens
    member = jnp.concatenate(
        [
            (slot == relative_int[tile : tile + 1]).astype(F32)
            for tile in range(tiles, 2 * tiles + 1)
        ],
        axis=1,
    ).astype(BF16)
    sums = dot(member, feature_ref[...])
    diagonal = (iota((tokens, LANES), 0) == iota((tokens, LANES), 1)).astype(F32)
    atoms_of = jnp.sum(diagonal * metas[1][4:5], axis=1, keepdims=True)
    token_out_ref[...] = (sums / atoms_of).astype(BF16)


def shards(
    atom_single,
    atom_token,
    token_atoms,
    window_offset,
    token_pair,
    w_zpair,
    w_single,
    w_pair_mlp,
    w_bias,
    w_attn,
    w_out,
    w_trans_in,
    w_trans_out,
    w_token,
):
    index, count = shard_place()
    atoms, width = atom_single.shape
    tokens, band, depth = token_pair.shape
    channels = w_zpair.shape[1]
    tiles = atoms // LANES
    pairs = tokens * band // LANES
    payload_rows = atoms + channels * pairs + 16

    local = (atom_token - (index - 1) * tokens).reshape(tiles, LANES)
    meta = jnp.concatenate(
        [
            local,
            jnp.pad(window_offset, (0, LANES - window_offset.shape[0]))[None],
            jnp.pad(token_atoms, (0, LANES - tokens))[None],
            jnp.zeros((16 - tiles - 2, LANES), jnp.int32),
        ],
        axis=0,
    ).astype(BF16)
    vmem = pl.BlockSpec(memory_space=pltpu.VMEM)
    payload = pl.pallas_call(
        project_kernel,
        out_shape=jax.ShapeDtypeStruct((payload_rows, width), BF16),
        in_specs=[vmem] * 4,
        out_specs=vmem,
        name="project",
    )(token_pair.reshape(tokens * band, depth), jnp.swapaxes(w_zpair, 0, 1), atom_single, meta)
    up = [(i, i + 1) for i in range(count - 1)]
    down = [(i + 1, i) for i in range(count - 1)]
    left = lax.ppermute(payload, RING, up)
    right = lax.ppermute(payload, RING, down)

    reach = 3 * atoms
    windows = (atoms + 5 * HALO) // QB
    heads = w_bias.shape[2]
    channels_out = w_token.shape[1]
    token_single, atom_out = pl.pallas_call(
        main_kernel,
        out_shape=(
            jax.ShapeDtypeStruct((tokens, channels_out), BF16),
            jax.ShapeDtypeStruct((atoms, width), BF16),
        ),
        in_specs=[vmem] * 11,
        out_specs=(vmem, vmem),
        scratch_shapes=[
            pltpu.VMEM((8, LANES), jnp.int32),
            pltpu.SMEM((8, LANES), jnp.int32),
            pltpu.VMEM((3 * tiles + 1, 8, LANES), jnp.int32),
            pltpu.VMEM((3 * tiles + 1, channels, LANES), F32),
            pltpu.VMEM((reach, LANES), jnp.int32),
            pltpu.VMEM((reach, LANES), jnp.int32),
            pltpu.VMEM((3 * pairs * channels, LANES), F32),
            pltpu.VMEM((channels, reach, LANES), F32),
            pltpu.VMEM((channels, LANES), F32),
            pltpu.VMEM((QB, LANES), jnp.int32),
            pltpu.VMEM((PAIR_SLOTS, 256, 256), F32),
            pltpu.VMEM((256, 256), F32),
            pltpu.VMEM((256, 256), BF16),
            pltpu.VMEM((256, 256), BF16),
            pltpu.VMEM((256, 256), BF16),
            pltpu.VMEM((256, 256), BF16),
            pltpu.VMEM((reach, 256), BF16),
            pltpu.VMEM((channels // 2, 256, 256), BF16),
            pltpu.VMEM((3, 256, 256), BF16),
            pltpu.VMEM((BLOCKS * heads * 256 // channels, 256), BF16),
            pltpu.VMEM((windows, BLOCKS, heads * QB, KW), F32),
            pltpu.VMEM((reach, width), F32),
            pltpu.VMEM((reach, LANES), F32),
            pltpu.VMEM((reach, width), BF16),
            pltpu.VMEM((reach, width), F32),
            pltpu.VMEM((reach, width), F32),
            pltpu.VMEM((reach, width), F32),
            pltpu.VMEM((reach, width), BF16),
            pltpu.VMEM((atoms + LANES, channels_out), BF16),
            pltpu.SemaphoreType.DMA,
        ],
        compiler_params=pltpu.CompilerParams(vmem_limit_bytes=48 * 2**20),
        name="encode",
    )(
        payload,
        left,
        right,
        jnp.swapaxes(w_single, 1, 2),
        w_pair_mlp,
        jnp.swapaxes(w_bias, 1, 2),
        w_attn,
        w_out,
        w_trans_in,
        w_trans_out,
        w_token,
    )
    return token_single, atom_out


def solution(mesh):
    split = ("group", "seq", "chan", "sub")
    in_specs = (
        P(split, None),
        P(split),
        P(split),
        P(split),
        P(split, None, None),
        P(),
        P(),
        P(),
        P(),
        P(),
        P(),
        P(),
        P(),
        P(),
    )
    out_specs = (P(split, None), P(split, None))
    return jax.shard_map(shards, mesh=mesh, in_specs=in_specs, out_specs=out_specs, check_vma=False)
```

time: 73 us -> 50.9 us (0.70)
  Pallas kernels: 56.7 us -> 34.3 us
  other arithmetic: 2.02 us -> 0.68 us
  waiting for transfers between devices: 3.17 us -> 4.09 us
    pallas_call x1, Pallas kernels: 53.3 us -> 30.9 us  [shards(): pl.pallas_call(main_kernel, out_shape=(jax.ShapeDtypeStruct((tokens, chan...]
    ppermute x1, waiting for transfers between devices: 0.75 us -> 1.67 us  [shards(): right = lax.ppermute(payload, RING, down)]
    unnamed x23 -> x24, local copies, waits for them, and re-layouts: 3.22 us -> 3.86 us
  transfers between devices with their start and end apart: 2 -> 2, of which waited for: 2 -> 2; matrix products, arithmetic and copies ran while one was open for 1% -> 0% of each run, Pallas kernels for 0% -> 0%
where the time goes in v2:
time: 50.9 us; the launch traced here: 50.3 us
  Pallas kernels  34.3 us (67%)
  starting transfers between devices  6.55 us (13%)
  waiting for transfers between devices  4.09 us (8%)
  local copies, waits for them, and re-layouts  3.94 us (8%)
  between operations  0.73 us (1%)
  other arithmetic  0.68 us (1%)
    pallas_call x1, Pallas kernels, shards(): pl.pallas_call(main_kernel, out_shape=(jax.ShapeDtypeStruct((tokens, chan...  30.9 us
    ppermute x1, starting transfers between devices, shards(): left = lax.ppermute(payload, RING, up)  4.46 us
    unnamed x24, local copies, waits for them, and re-layouts  3.86 us
    pallas_call x1, Pallas kernels, shards(): pl.pallas_call(project_kernel, out_shape=jax.ShapeDtypeStruct((payload_ro...  3.38 us
    ppermute x1, waiting for transfers between devices, shards(): left = lax.ppermute(payload, RING, up)  2.42 us
    ppermute x1, starting transfers between devices, shards(): right = lax.ppermute(payload, RING, down)  2.09 us
    ppermute x1, waiting for transfers between devices, shards(): right = lax.ppermute(payload, RING, down)  1.67 us
  transfers between devices with their start and end apart: 2, of which 2 were waited for; matrix products, arithmetic and copies ran while one was open for 0% of the time, Pallas kernels for 0%

profile of v2, /device:TPU:1, one launch (start us, length us, event | category | flops | bytes accessed | tf_op | source)
XLA Modules:
  0.0 50.3 jit_solution(14840342978306635001)
XLA Ops:
  0.6 0.0 copy-start.10
  0.6 0.6 %copy-done.10 = s32[48]{0:T(128)S(1)} copy-done((s32[48]{0:T(128)S(1)}, s32[48]{0:T(128)}, u32[]{:S(2)}) %copy-start.10) | copy-done | bytes 216
  1.3 0.0 copy-start.11
  1.3 0.6 %copy-done.11 = s32[12]{0:T(128)S(1)} copy-done((s32[12]{0:T(128)S(1)}, s32[12]{0:T(128)}, u32[]{:S(2)}) %copy-start.11) | copy-done | bytes 72
  2.0 0.0 copy-start.9
  2.0 0.7 %copy-done.9 = s32[384]{0:T(512)S(1)} copy-done((s32[384]{0:T(512)S(1)}, s32[384]{0:T(512)}, u32[]{:S(2)}) %copy-start.9) | copy-done | bytes 1560
  2.7 0.1 pad.15.clone
  2.7 0.0 copy-start.7
  2.7 0.7 %maximum_maximum_fusion.meta_ref = bf16[16,128]{1,0:T(8,128)(2,1)} fusion(bf16[1,128]{1,0:T(2,128)(2,1)S(1)} %get-tuple-element.2, bf16[1,128]{1,0:T(2,128)(2,1)S(1)} %get-tuple-element.3, bf16[3,128]{1,0:T(4,128)(2,1)S(1)} %fusion, bf16[16]{0:T(256)(128)(2,1)S(1)} %pad.15.clone), kind=kLoop, calls=%fused_computation | loop fusion | flops 16384 | bytes 5408 | tf_op jit(solution)/shard_map/concatenate | solution.py:439
  3.4 0.0 copy-start.1
  3.4 0.0 copy-start.2
  3.4 0.0 copy-start.3
  3.4 0.0 copy-start.5
  3.4 0.0 copy-start.6
  3.4 3.4 %project.1.own_ref = bf16[784,128]{1,0:T(8,128)(2,1)} custom-call(bf16[3072,128]{1,0:T(8,128)(2,1)} %bitcast.12, bf16[16,128]{1,0:T(8,128)(2,1)} %bitcast.13, bf16[384,128]{1,0:T(8,128)(2,1)} %atom_ref.1, bf16[16,128]{1,0:T(8,128)(2,1)} %maximum_maximum_fusion.meta_ref), custom_call_target="tpu_custom_call" | custom-call | tf_op jit(solution)/shard_map/project/pallas_call | solution.py:449
  6.8 0.0 copy-start.8
  6.8 2.1 %collective-permute-start.1 = (bf16[784,128]{1,0:T(8,128)(2,1)}, bf16[784,128]{1,0:T(8,128)(2,1)S(1)}, u32[]{:S(2)}, u32[]{:S(2)}) collective-permute-start(bf16[784,128]{1,0:T(8,128)(2,1)} %project.1.own_ref), channel_id=1, source_target_pairs={{1,0},{2,1},{3,2},{4,3},{5,4},{6,5},{7,6},{8,7},{9,8},{10,9},{11,1... | collective-permute-start | bytes 602120 | tf_op jit(solution)/shard_map/ppermute | solution.py:459
  8.9 4.5 %collective-permute-start = (bf16[784,128]{1,0:T(8,128)(2,1)}, bf16[784,128]{1,0:T(8,128)(2,1)S(1)}, u32[]{:S(2)}, u32[]{:S(2)}) collective-permute-start(bf16[784,128]{1,0:T(8,128)(2,1)} %project.1.own_ref), channel_id=1, source_target_pairs={{0,1},{1,2},{2,3},{3,4},{4,5},{5,6},{6,7},{7,8},{8,9},{9,10},{10,1... | collective-permute-start | bytes 602120 | tf_op jit(solution)/shard_map/ppermute | solution.py:458
  13.4 1.7 %collective-permute-done.1.right_ref = bf16[784,128]{1,0:T(8,128)(2,1)S(1)} collective-permute-done((bf16[784,128]{1,0:T(8,128)(2,1)}, bf16[784,128]{1,0:T(8,128)(2,1)S(1)}, u32[]{:S(2)}, u32[]{:S(2)}) %collective-permute-start.1) | collective-permute-done | bytes 200736 | tf_op jit(solution)/shard_map/ppermute | solution.py:459
  15.0 2.4 %collective-permute-done.left_ref = bf16[784,128]{1,0:T(8,128)(2,1)S(1)} collective-permute-done((bf16[784,128]{1,0:T(8,128)(2,1)}, bf16[784,128]{1,0:T(8,128)(2,1)S(1)}, u32[]{:S(2)}, u32[]{:S(2)}) %collective-permute-start) | collective-permute-done | bytes 200736 | tf_op jit(solution)/shard_map/ppermute | solution.py:458
  17.5 0.0 copy-done.7
  17.5 0.0 copy-done.1
  17.5 0.0 copy-done.2
  17.5 0.0 copy-done.3
  17.5 0.0 copy-done.5
  17.5 0.0 copy-done.6
  17.5 0.0 copy-done.8
  17.5 0.0 copy-start
  17.5 0.9 %copy-done = bf16[784,128]{1,0:T(8,128)(2,1)S(1)} copy-done((bf16[784,128]{1,0:T(8,128)(2,1)S(1)}, bf16[784,128]{1,0:T(8,128)(2,1)}, u32[]{:S(2)}) %copy-start) | copy-done | bytes 200728
  18.4 0.0 copy-start.4
  18.4 0.9 %copy-done.4 = bf16[128,768]{1,0:T(8,128)(2,1)S(1)} copy-done((bf16[128,768]{1,0:T(8,128)(2,1)S(1)}, bf16[128,768]{1,0:T(8,128)(2,1)}, u32[]{:S(2)}) %copy-start.4) | copy-done | bytes 196632
  19.4 30.9 %encode.1 = (bf16[48,768]{1,0:T(8,128)(2,1)}, bf16[384,128]{1,0:T(8,128)(2,1)}) custom-call(bf16[784,128]{1,0:T(8,128)(2,1)S(1)} %copy-done, bf16[784,128]{1,0:T(8,128)(2,1)S(1)} %collective-permute-done.left_ref, bf16[784,128]{1,0:T(8,128)(2,1)S(1)} %collective-permute-done.1.right_ref, bf16[2,16,128]{2,1,0:T(8,128)(2,1)S(1)} %bitcast.10, ...), custom_call_target="tpu_custom_call" | custom-call | tf_op jit(solution)/shard_map/encode/pallas_call | solution.py:465
  (5 shorter events, 0.0 us)
Async XLA Ops:
  0.6 0.7 %copy-start.10 = (s32[48]{0:T(128)S(1)}, s32[48]{0:T(128)}, u32[]{:S(2)}) copy-start(s32[48]{0:T(128)} %param.16) | copy-start | bytes 580
  1.3 0.7 %copy-start.11 = (s32[12]{0:T(128)S(1)}, s32[12]{0:T(128)}, u32[]{:S(2)}) copy-start(s32[12]{0:T(128)} %param.17) | copy-start | bytes 148
  2.0 0.7 %copy-start.9 = (s32[384]{0:T(512)S(1)}, s32[384]{0:T(512)}, u32[]{:S(2)}) copy-start(s32[384]{0:T(512)} %param.15) | copy-start | bytes 4612
  2.7 14.7 %copy-start.7 = (bf16[2,128,16]{1,2,0:T(8,128)(2,1)S(1)}, bf16[2,128,16]{1,2,0:T(8,128)(2,1)}, u32[]{:S(2)}) copy-start(bf16[2,128,16]{1,2,0:T(8,128)(2,1)} %param.20) | copy-start | bytes 24580
  3.4 14.1 %copy-start.1 = (bf16[3,4,128,128]{3,2,1,0:T(8,128)(2,1)S(1)}, bf16[3,4,128,128]{3,2,1,0:T(8,128)(2,1)}, u32[]{:S(2)}) copy-start(bf16[3,4,128,128]{3,2,1,0:T(8,128)(2,1)} %w_attn_ref.1) | copy-start | bytes 1179652
  3.4 14.1 %copy-start.2 = (bf16[3,2,128,256]{3,2,1,0:T(8,128)(2,1)S(1)}, bf16[3,2,128,256]{3,2,1,0:T(8,128)(2,1)}, u32[]{:S(2)}) copy-start(bf16[3,2,128,256]{3,2,1,0:T(8,128)(2,1)} %w_in_ref.1) | copy-start | bytes 1179652
  3.4 14.1 %copy-start.3 = (bf16[3,256,128]{2,1,0:T(8,128)(2,1)S(1)}, bf16[3,256,128]{2,1,0:T(8,128)(2,1)}, u32[]{:S(2)}) copy-start(bf16[3,256,128]{2,1,0:T(8,128)(2,1)} %w_trans_out_ref.1) | copy-start | bytes 589828
  3.4 14.1 %copy-start.5 = (bf16[3,128,128]{2,1,0:T(8,128)(2,1)S(1)}, bf16[3,128,128]{2,1,0:T(8,128)(2,1)}, u32[]{:S(2)}) copy-start(bf16[3,128,128]{2,1,0:T(8,128)(2,1)} %w_out_ref.1) | copy-start | bytes 294916
  3.4 14.1 %copy-start.6 = (bf16[3,16,16]{2,1,0:T(8,128)(2,1)S(1)}, bf16[3,16,16]{2,1,0:T(8,128)(2,1)}, u32[]{:S(2)}) copy-start(bf16[3,16,16]{2,1,0:T(8,128)(2,1)} %w_mlp_ref.1) | copy-start | bytes 4612
  6.8 10.7 %copy-start.8 = (bf16[3,16,4]{1,2,0:T(4,128)(2,1)S(1)}, bf16[3,16,4]{1,2,0:T(4,128)(2,1)}, u32[]{:S(2)}) copy-start(bf16[3,16,4]{1,2,0:T(4,128)(2,1)} %param.22) | copy-start | bytes 1156
  6.8 8.2 %collective-permute-start.1 = (bf16[784,128]{1,0:T(8,128)(2,1)}, bf16[784,128]{1,0:T(8,128)(2,1)S(1)}, u32[]{:S(2)}, u32[]{:S(2)}) collective-permute-start(bf16[784,128]{1,0:T(8,128)(2,1)} %project.1.own_ref), channel_id=1, source_target_pairs={{1,0},{2,1},{3,2},{4,3},{5,4},{6,5},{7,6},{8,7},{9,8},{10,9},{11,1... | collective-permute-start | bytes 602120 | tf_op jit(solution)/shard_map/ppermute | solution.py:459
  8.9 8.6 %collective-permute-start = (bf16[784,128]{1,0:T(8,128)(2,1)}, bf16[784,128]{1,0:T(8,128)(2,1)S(1)}, u32[]{:S(2)}, u32[]{:S(2)}) collective-permute-start(bf16[784,128]{1,0:T(8,128)(2,1)} %project.1.own_ref), channel_id=1, source_target_pairs={{0,1},{1,2},{2,3},{3,4},{4,5},{5,6},{6,7},{7,8},{8,9},{9,10},{10,1... | collective-permute-start | bytes 602120 | tf_op jit(solution)/shard_map/ppermute | solution.py:458
  17.5 0.9 %copy-start = (bf16[784,128]{1,0:T(8,128)(2,1)S(1)}, bf16[784,128]{1,0:T(8,128)(2,1)}, u32[]{:S(2)}) copy-start(bf16[784,128]{1,0:T(8,128)(2,1)} %project.1.own_ref) | copy-start | bytes 602116
  18.4 0.9 %copy-start.4 = (bf16[128,768]{1,0:T(8,128)(2,1)S(1)}, bf16[128,768]{1,0:T(8,128)(2,1)}, u32[]{:S(2)}) copy-start(bf16[128,768]{1,0:T(8,128)(2,1)} %w_token_ref.1) | copy-start | bytes 589828

commit v3 on v2

--- a/solution.py
+++ b/solution.py
@@ -12,9 +12,9 @@
 KW = 128
 HALO = 96
 LANES = 128
-PAIR_DEPTH = 6
+PAIR_DEPTH = 4
 PAIR_SLOTS = 4
-PAIR_UNROLL = 3
+PAIR_GROUP = 3
 EPSILON = 1e-05
 RING = ("seq", "chan", "sub")
 NT = (((1,), (1,)), ((), ()))
@@ -49,31 +49,111 @@
     return shifted * lax.rsqrt(spread + EPSILON)
 
 
-def project_kernel(pair_ref, wz_ref, atom_ref, meta_ref, out_ref):
+def project_kernel(
+    pair_hbm,
+    wz_hbm,
+    atom_hbm,
+    token_hbm,
+    atoms_of_hbm,
+    offset_hbm,
+    out_hbm,
+    pair_ref,
+    wz_ref,
+    token_ref,
+    atoms_of_ref,
+    offset_ref,
+    band_ref,
+    meta_ref,
+    small_sems,
+    in_sems,
+    out_sems,
+):
     rows, width = pair_ref.shape
-    atoms = atom_ref.shape[0]
-    channels = wz_ref.shape[0]
+    atoms = atom_hbm.shape[0]
+    tokens = atoms_of_hbm.shape[0]
+    channels = wz_hbm.shape[0]
+    tiles = atoms // LANES
+    parts = in_sems.shape[0]
+    step = rows // parts
+    band_step = channels * step // LANES
+    meta = atoms + channels * rows // LANES
+
+    loads = [
+        pltpu.make_async_copy(
+            pair_hbm.at[pl.ds(step * part, step)],
+            pair_ref.at[pl.ds(step * part, step)],
+            in_sems.at[part],
+        )
+        for part in range(parts)
+    ]
+    small = [
+        pltpu.make_async_copy(wz_hbm, wz_ref, small_sems.at[0]),
+        pltpu.make_async_copy(token_hbm, token_ref, small_sems.at[1]),
+        pltpu.make_async_copy(atoms_of_hbm, atoms_of_ref, small_sems.at[2]),
+        pltpu.make_async_copy(offset_hbm, offset_ref, small_sems.at[3]),
+    ]
+    atom_copy = pltpu.make_async_copy(atom_hbm, out_hbm.at[pl.ds(0, atoms)], out_sems.at[parts])
+    loads[0].start()
+    for copy in small + loads[1:]:
+        copy.start()
+    atom_copy.start()
+
     eye = iota((width, width), 0) == iota((width, width), 1)
     centring = (eye.astype(F32) - 1.0 / width).astype(BF16)
     average = jnp.full((channels, width), 1.0 / width, BF16)
-    step = 512
-    for first in range(0, rows, step):
-        shifted = dot(pair_ref[first : first + step, :], centring)
+    for copy in small:
+        copy.wait()
+    index, _ = shard_place()
+    meta_ref[...] = jnp.zeros_like(meta_ref)
+    base = (index - 1) * tokens
+    for tile in range(tiles):
+        local = token_ref[LANES * tile : LANES * (tile + 1)].reshape(1, LANES) - base
+        meta_ref[tile : tile + 1, :] = local.astype(F32)
+    meta_ref[tiles : tiles + 1, 0 : offset_ref.shape[0]] = (
+        offset_ref[...].reshape(1, offset_ref.shape[0]).astype(F32)
+    )
+    meta_ref[tiles + 1 : tiles + 2, 0:tokens] = (
+        atoms_of_ref[...].reshape(1, tokens).astype(F32)
+    )
+    band_ref[meta - atoms :, :] = meta_ref[...].astype(BF16)
+    stores = []
+    for part in range(parts):
+        loads[part].wait()
+        shifted = dot(pair_ref[step * part : step * (part + 1), :], centring)
         spread = dot_nt(average, (shifted * shifted).astype(BF16))
         projected = dot_nt(wz_ref[...], shifted.astype(BF16))
         projected = (projected * lax.rsqrt(spread + EPSILON)).astype(BF16)
-        for part in range(step // LANES):
-            row = atoms + channels * ((first // LANES) + part)
-            out_ref[row : row + channels, :] = projected[:, LANES * part : LANES * (part + 1)]
-    out_ref[0:atoms, :] = atom_ref[...]
-    row = atoms + channels * (rows // LANES)
-    out_ref[row : row + 16, :] = meta_ref[...]
+        for tile in range(step // LANES):
+            row = band_step * part + channels * tile
+            band_ref[row : row + channels, :] = projected[:, LANES * tile : LANES * (tile + 1)]
+        first, count = band_step * part, band_step + (16 if part == parts - 1 else 0)
+        copy = pltpu.make_async_copy(
+            band_ref.at[pl.ds(first, count)],
+            out_hbm.at[pl.ds(atoms + first, count)],
+            out_sems.at[part],
+        )
+        copy.start()
+        stores.append(copy)
+    for copy in stores:
+        copy.wait()
+    atom_copy.wait()
 
 
 def main_kernel(
-    own_ref,
-    left_ref,
-    right_ref,
+    own_hbm,
+    near_hbm,
+    far_hbm,
+    w_single_hbm,
+    w_mlp_hbm,
+    w_bias_hbm,
+    w_attn_hbm,
+    w_out_hbm,
+    w_in_hbm,
+    w_trans_out_hbm,
+    w_token_hbm,
+    token_out_ref,
+    atom_out_ref,
+    payload_ref,
     w_single_ref,
     w_mlp_ref,
     w_bias_ref,
@@ -82,8 +162,6 @@
     w_in_ref,
     w_trans_out_ref,
     w_token_ref,
-    token_out_ref,
-    atom_out_ref,
     scalars_vmem,
     scalars,
     token_rows,
@@ -95,8 +173,6 @@
     side_ref,
     column_ref,
     start_ref,
-    pair_ref,
-    first_ref,
     second_ref,
     third_ref,
     normed_ref,
@@ -113,7 +189,8 @@
     value_ref,
     gated_ref,
     feature_ref,
-    sem,
+    sems,
+    weight_sems,
 ):
     index, count = shard_place()
     atoms, width = atom_out_ref.shape
@@ -130,27 +207,31 @@
     window_count = (atoms + HALO + 4 * HALO) // QB
     query_end = first_query + QB * window_count
 
-    sides = (left_ref, own_ref, right_ref)
-    metas = [ref[meta : meta + 16, :].astype(F32) for ref in sides]
-    number = iota((3 * tiles, LANES), 0) * LANES + iota((3 * tiles, LANES), 1)
-    relative = jnp.concatenate(
-        [m[0:tiles] + s for m, s in zip(metas, (-tokens, 0, tokens))], axis=0
-    )
-    inside = (number >= first_valid) & (number < end_valid)
-    relative = jnp.where(inside, relative, -64.0)
-    relative_int = relative.astype(jnp.int32)
-    offset_lanes = atoms // QB
-    offset_row = (
-        metas[0][3:4]
-        + pltpu.roll(metas[1][3:4], offset_lanes, 1)
-        + pltpu.roll(metas[2][3:4], 2 * offset_lanes, 1)
-    )
-    scalars_vmem[...] = jnp.broadcast_to(offset_row, (8, LANES)).astype(jnp.int32)
-    copy = pltpu.make_async_copy(scalars_vmem, scalars, sem)
-    copy.start()
-    for tile in range(3 * tiles):
-        token_rows[tile] = jnp.broadcast_to(relative_int[tile : tile + 1], (8, LANES))
-    token_rows[3 * tiles] = jnp.zeros((8, LANES), jnp.int32)
+    even = index % 2 == 0
+    copies = [
+        pltpu.make_async_copy(own_hbm, payload_ref.at[1], sems.at[0]),
+        pltpu.make_async_copy(near_hbm, payload_ref.at[jnp.where(even, 2, 0)], sems.at[1]),
+        pltpu.make_async_copy(far_hbm, payload_ref.at[jnp.where(even, 0, 2)], sems.at[2]),
+    ]
+    weight_copies = [
+        pltpu.make_async_copy(source, target, weight_sems.at[i])
+        for i, (source, target) in enumerate(
+            (
+                (w_mlp_hbm, w_mlp_ref),
+                (w_bias_hbm, w_bias_ref),
+                (w_single_hbm, w_single_ref),
+                (w_attn_hbm, w_attn_ref),
+                (w_out_hbm, w_out_ref),
+                (w_in_hbm, w_in_ref),
+                (w_trans_out_hbm, w_trans_out_ref),
+                (w_token_hbm, w_token_ref),
+            )
+        )
+    ]
+    for copy in weight_copies[:3] + copies + weight_copies[3:]:
+        copy.start()
+    for copy in weight_copies[:3]:
+        copy.wait()
 
     big = 256
     group = big // channels
@@ -166,6 +247,30 @@
         bias_weight_ref[layer * per_block : (layer + 1) * per_block, :] = jnp.where(
             same_query[0:per_block], dot_nt(by_row, select), 0.0
         ).astype(BF16)
+
+    for copy in copies:
+        copy.wait()
+    sides = tuple(payload_ref.at[side] for side in range(3))
+    metas = [ref[meta : meta + 16, :].astype(F32) for ref in sides]
+    number = iota((3 * tiles, LANES), 0) * LANES + iota((3 * tiles, LANES), 1)
+    relative = jnp.concatenate(
+        [m[0:tiles] + s for m, s in zip(metas, (-tokens, 0, tokens))], axis=0
+    )
+    inside = (number >= first_valid) & (number < end_valid)
+    relative = jnp.where(inside, relative, -64.0)
+    relative_int = relative.astype(jnp.int32)
+    offset_lanes = atoms // QB
+    offset_row = (
+        metas[0][3:4]
+        + pltpu.roll(metas[1][3:4], offset_lanes, 1)
+        + pltpu.roll(metas[2][3:4], 2 * offset_lanes, 1)
+    )
+    scalars_vmem[...] = jnp.broadcast_to(offset_row, (8, LANES)).astype(jnp.int32)
+    copy = pltpu.make_async_copy(scalars_vmem, scalars, sems.at[3])
+    copy.start()
+    for tile in range(3 * tiles):
+        token_rows[tile] = jnp.broadcast_to(relative_int[tile : tile + 1], (8, LANES))
+    token_rows[3 * tiles] = jnp.zeros((8, LANES), jnp.int32)
 
     eye = iota((LANES, LANES), 0) == iota((LANES, LANES), 1)
     ones = jnp.ones((LANES, LANES), BF16)
@@ -231,11 +336,8 @@
     def key_start(n):
         return HALO + QB * n + scalars[0, n + offset_lanes - 2 * HALO // QB]
 
-    def window_of(step, behind):
-        return jnp.clip(step - behind, 0, window_count - 1)
-
-    def column_stage(step):
-        n = window_of(step, 0)
+    def column_stage(step, w):
+        n = (step * PAIR_GROUP + w)
         query = pl.multiple_of(first_query + QB * n, QB)
         start = key_start(n)
         tile = start // LANES
@@ -244,77 +346,97 @@
         key_tokens = pltpu.roll(
             jnp.where(lane8 >= shift, token_rows[tile], token_rows[tile + 1]), back, 1
         )
-        side_ref[...] = pltpu.roll(
+        side_ref[w] = pltpu.roll(
             jnp.where(lane >= shift, key_terms[tile], key_terms[tile + 1]), back, 1
         )
         for g in range(QB // 8):
             rows = pl.ds(query + 8 * g, 8)
-            column_ref[8 * g : 8 * g + 8, :] = (
+            column_ref[w, 8 * g : 8 * g + 8, :] = (
                 jnp.clip(key_tokens + token_shift[rows, :], 0, LANES // 2 - 1)
                 + token_base[rows, :]
             )
 
-    def start_stage(step):
-        query = pl.multiple_of(first_query + QB * window_of(step, 1), QB)
+    def start_stage(step, w):
+        query = pl.multiple_of(first_query + QB * (step * PAIR_GROUP + w), QB)
         slot = step % PAIR_SLOTS
+        for g in range(QB // 8):
+            half, part = g // (group // 8), g % (group // 8)
+            at = slice(half * LANES, (half + 1) * LANES)
+            column = column_ref[w, 8 * g : 8 * g + 8, :]
+            rows = pl.ds(query + 8 * g, 8)
+            for e in range(channels):
+                row = e * group + 8 * part
+                start_ref[slot, w, row : row + 8, at] = jnp.take_along_axis(
+                    band_ref[e, rows, :], column, axis=1, mode="promise_in_bounds"
+                ) + jnp.broadcast_to(side_ref[w, e : e + 1, :], (8, LANES))
+
+    def relu(values):
+        return jnp.maximum(values.astype(BF16), jnp.zeros((), BF16))
+
+    def first_stage(step, w):
+        slot = (step + 3) % PAIR_SLOTS
+        second_ref[w] = relu(dot(mlp_ref[0], relu(start_ref[slot, w])))
+
+    def second_stage(w):
+        third_ref[w] = relu(dot(mlp_ref[1], second_ref[w]))
+
+    def norm_stage(step, w):
+        slot = (step + 1) % PAIR_SLOTS
+        third = dot(mlp_ref[2], third_ref[w])
         for half in range(2):
             at = slice(half * LANES, (half + 1) * LANES)
-            pieces = [[] for _ in range(channels)]
-            for g in range(half * group // 8, (half + 1) * group // 8):
-                column = column_ref[8 * g : 8 * g + 8, :]
-                rows = pl.ds(query + 8 * g, 8)
-                for e in range(channels):
-                    pieces[e].append(
-                        jnp.take_along_axis(
-                            band_ref[e, rows, :], column, axis=1, mode="promise_in_bounds"
-                        )
-                        + jnp.broadcast_to(side_ref[e : e + 1, :], (8, LANES))
-                    )
+            normed = []
+            for part in range(group // 8):
+                pair = [
+                    third[e * group + 8 * part : e * group + 8 * part + 8, at]
+                    + start_ref[slot, w, e * group + 8 * part : e * group + 8 * part + 8, at]
+                    for e in range(channels)
+                ]
+                centre = sum(pair[1:], pair[0]) * (1.0 / channels)
+                shifted = [p - centre for p in pair]
+                spread = sum([s * s for s in shifted[1:]], shifted[0] * shifted[0])
+                factor = lax.rsqrt(spread * (1.0 / channels) + EPSILON) * log2e
+                normed.append([s * factor for s in shifted])
             for e in range(channels):
-                piece = jnp.concatenate(pieces[e], axis=0)
-                start_ref[slot, e * group : (e + 1) * group, at] = piece
-                first_ref[e * group : (e + 1) * group, at] = jnp.maximum(
-                    piece.astype(BF16), jnp.zeros((), BF16)
-                )
-
-    def hidden_stage(layer, from_ref, to_ref):
-        hidden = dot(mlp_ref[layer], from_ref[...]).astype(BF16)
-        to_ref[...] = jnp.maximum(hidden, jnp.zeros((), BF16))
-
-    def sum_stage(step):
-        pair_ref[...] = start_ref[(step + 1) % PAIR_SLOTS] + dot(mlp_ref[2], third_ref[...])
-
-    def norm_stage():
-        for half in range(2):
-            at = slice(half * LANES, (half + 1) * LANES)
-            pair = pair_ref[:, at].reshape(channels, group, LANES)
-            shifted = pair - jnp.mean(pair, axis=0, keepdims=True)
-            spread = jnp.mean(shifted * shifted, axis=0, keepdims=True)
-            normed = shifted * (lax.rsqrt(spread + EPSILON) * log2e)
-            normed_ref[:, at] = normed.reshape(big, LANES).astype(BF16)
-
-    def bias_stage(step):
-        n = window_of(step, PAIR_DEPTH)
-        bias = dot(bias_weight_ref[...], normed_ref[...])
+                rows = jnp.concatenate([n[e] for n in normed], axis=0)
+                normed_ref[w, e * group : (e + 1) * group, at] = rows.astype(BF16)
+
+    def bias_stage(step, w):
+        n = (step - PAIR_DEPTH) * PAIR_GROUP + w
+        bias = dot(bias_weight_ref[...], normed_ref[w])
         for layer in range(BLOCKS):
             part = bias[layer * per_block : (layer + 1) * per_block]
             bias_ref[n, layer, 0:per_block, :] = part[:, 0:LANES]
             bias_ref[n, layer, per_block : 2 * per_block, :] = part[:, LANES:]
 
-    def pair_step(outer, carry):
-        for inner in range(PAIR_UNROLL):
-            step = outer * PAIR_UNROLL + inner
-            bias_stage(step)
-            norm_stage()
-            sum_stage(step)
-            hidden_stage(1, second_ref, third_ref)
-            hidden_stage(0, first_ref, second_ref)
-            start_stage(step)
-            column_stage(step)
+    groups = window_count // PAIR_GROUP
+
+    def pair_step(step, carry=None):
+        def live(behind):
+            return not isinstance(step, int) or 0 <= step - behind < groups
+
+        for w in range(PAIR_GROUP):
+            if live(4):
+                bias_stage(step, w)
+            if live(3):
+                norm_stage(step, w)
+            if live(2):
+                second_stage(w)
+            if live(1):
+                first_stage(step, w)
+            if live(0):
+                column_stage(step, w)
+                start_stage(step, w)
         return carry
 
-    lax.fori_loop(0, -(-(window_count + PAIR_DEPTH) // PAIR_UNROLL), pair_step, 0)
-
+    for step in range(PAIR_DEPTH):
+        pair_step(step)
+    lax.fori_loop(PAIR_DEPTH, groups, pair_step, 0)
+    for step in range(groups, groups + PAIR_DEPTH):
+        pair_step(step)
+
+    for copy in weight_copies[3:]:
+        copy.wait()
     head_of_lane = iota((QB // 2, width), 1) // head_size
     scale = log2e / math.sqrt(head_size)
 
@@ -435,29 +557,51 @@
     pairs = tokens * band // LANES
     payload_rows = atoms + channels * pairs + 16
 
-    local = (atom_token - (index - 1) * tokens).reshape(tiles, LANES)
-    meta = jnp.concatenate(
-        [
-            local,
-            jnp.pad(window_offset, (0, LANES - window_offset.shape[0]))[None],
-            jnp.pad(token_atoms, (0, LANES - tokens))[None],
-            jnp.zeros((16 - tiles - 2, LANES), jnp.int32),
-        ],
-        axis=0,
-    ).astype(BF16)
     vmem = pl.BlockSpec(memory_space=pltpu.VMEM)
+    anywhere = pl.BlockSpec(memory_space=pl.ANY)
+    parts = 3
     payload = pl.pallas_call(
         project_kernel,
         out_shape=jax.ShapeDtypeStruct((payload_rows, width), BF16),
-        in_specs=[vmem] * 4,
-        out_specs=vmem,
+        in_specs=[anywhere] * 6,
+        out_specs=anywhere,
+        scratch_shapes=[
+            pltpu.VMEM((tokens * band, depth), BF16),
+            pltpu.VMEM((channels, depth), BF16),
+            pltpu.VMEM((atoms,), jnp.int32),
+            pltpu.VMEM((tokens,), jnp.int32),
+            pltpu.VMEM(window_offset.shape, jnp.int32),
+            pltpu.VMEM((payload_rows - atoms, width), BF16),
+            pltpu.VMEM((16, width), F32),
+            pltpu.SemaphoreType.DMA((4,)),
+            pltpu.SemaphoreType.DMA((parts,)),
+            pltpu.SemaphoreType.DMA((parts + 1,)),
+        ],
         name="project",
-    )(token_pair.reshape(tokens * band, depth), jnp.swapaxes(w_zpair, 0, 1), atom_single, meta)
-    up = [(i, i + 1) for i in range(count - 1)]
-    down = [(i + 1, i) for i in range(count - 1)]
-    left = lax.ppermute(payload, RING, up)
-    right = lax.ppermute(payload, RING, down)
-
+    )(
+        token_pair.reshape(tokens * band, depth),
+        jnp.swapaxes(w_zpair, 0, 1),
+        atom_single,
+        atom_token,
+        token_atoms,
+        window_offset,
+    )
+    near = [(i, i ^ 1) for i in range(count)]
+    far = [(i, ((i + 1) ^ 1) - 1) for i in range(1, count - 1)]
+    first_side = lax.ppermute(payload, RING, near)
+    second_side = lax.ppermute(payload, RING, far)
+
+    weights = (
+        jnp.swapaxes(w_single, 1, 2),
+        w_pair_mlp,
+        jnp.swapaxes(w_bias, 1, 2),
+        w_attn,
+        w_out,
+        w_trans_in,
+        w_trans_out,
+        w_token,
+    )
+    in_hbm = pl.BlockSpec(memory_space=pltpu.HBM)
     reach = 3 * atoms
     windows = (atoms + 5 * HALO) // QB
     heads = w_bias.shape[2]
@@ -468,9 +612,11 @@
             jax.ShapeDtypeStruct((tokens, channels_out), BF16),
             jax.ShapeDtypeStruct((atoms, width), BF16),
         ),
-        in_specs=[vmem] * 11,
+        in_specs=[in_hbm] + [anywhere] * 2 + [in_hbm] * len(weights),
         out_specs=(vmem, vmem),
         scratch_shapes=[
+            pltpu.VMEM((3, payload_rows, width), BF16),
+            *[pltpu.VMEM(w.shape, BF16) for w in weights],
             pltpu.VMEM((8, LANES), jnp.int32),
             pltpu.SMEM((8, LANES), jnp.int32),
             pltpu.VMEM((3 * tiles + 1, 8, LANES), jnp.int32),
@@ -479,14 +625,10 @@
             pltpu.VMEM((reach, LANES), jnp.int32),
             pltpu.VMEM((3 * pairs * channels, LANES), F32),
             pltpu.VMEM((channels, reach, LANES), F32),
-            pltpu.VMEM((channels, LANES), F32),
-            pltpu.VMEM((QB, LANES), jnp.int32),
-            pltpu.VMEM((PAIR_SLOTS, 256, 256), F32),
-            pltpu.VMEM((256, 256), F32),
-            pltpu.VMEM((256, 256), BF16),
-            pltpu.VMEM((256, 256), BF16),
-            pltpu.VMEM((256, 256), BF16),
-            pltpu.VMEM((256, 256), BF16),
+            pltpu.VMEM((PAIR_GROUP, channels, LANES), F32),
+            pltpu.VMEM((PAIR_GROUP, QB, LANES), jnp.int32),
+            pltpu.VMEM((PAIR_SLOTS, PAIR_GROUP, 256, 256), F32),
+            *[pltpu.VMEM((PAIR_GROUP, 256, 256), BF16)] * 3,
             pltpu.VMEM((reach, 256), BF16),
             pltpu.VMEM((channels // 2, 256, 256), BF16),
             pltpu.VMEM((3, 256, 256), BF16),
@@ -500,22 +642,16 @@
             pltpu.VMEM((reach, width), F32),
             pltpu.VMEM((reach, width), BF16),
             pltpu.VMEM((atoms + LANES, channels_out), BF16),
-            pltpu.SemaphoreType.DMA,
+            pltpu.SemaphoreType.DMA((4,)),
+            pltpu.SemaphoreType.DMA((len(weights),)),
         ],
         compiler_params=pltpu.CompilerParams(vmem_limit_bytes=48 * 2**20),
         name="encode",
     )(
-        payload,
-        left,
-        right,
-        jnp.swapaxes(w_single, 1, 2),
-        w_pair_mlp,
-        jnp.swapaxes(w_bias, 1, 2),
-        w_attn,
-        w_out,
-        w_trans_in,
-        w_trans_out,
-        w_token,
+        pltpu.with_memory_space_constraint(payload, pltpu.HBM),
+        first_side,
+        second_side,
+        *[pltpu.with_memory_space_constraint(w, pltpu.HBM) for w in weights],
     )
     return token_single, atom_out
 

time: 50.9 us -> 43.5 us (0.85)
  local copies, waits for them, and re-layouts: 3.94 us -> 0 us
  starting transfers between devices: 6.55 us -> 4.58 us
  Pallas kernels: 34.3 us -> 33 us
  waiting for transfers between devices: 4.09 us -> 5.03 us
  other arithmetic: 0.68 us -> 0 us
    unnamed x24 -> x0, local copies, waits for them, and re-layouts: 3.86 us -> none
    pallas_call x1, Pallas kernels: 30.9 us -> 28.8 us  [shards(): pl.pallas_call(main_kernel, out_shape=(jax.ShapeDtypeStruct((tokens, chan...]
    ppermute x2, starting transfers between devices: 6.55 us -> 4.58 us  [the longest x1 4.51 us: shards(): second_side = lax.ppermute(payload, RING, far)]
    ppermute x2, waiting for transfers between devices: 4.09 us -> 5.03 us  [the longest x1 5.02 us: shards(): second_side = lax.ppermute(payload, RING, far)]
    pallas_call x1, Pallas kernels: 3.38 us -> 4.19 us  [shards(): pl.pallas_call(project_kernel, out_shape=jax.ShapeDtypeStruct((payload_ro...]
    concatenate x1 -> x0, other arithmetic: 0.67 us -> none  [shards(): jnp.concatenate([local, jnp.pad(window_offset, (0, LANES - window_offset....]
  transfers between devices with their start and end apart: 2 -> 2, of which waited for: 2 -> 1; matrix products, arithmetic and copies ran while one was open for 0% -> 0% of each run, Pallas kernels for 0% -> 0%
where the time goes in v3:
time: 43.5 us; the launch traced here: 43.3 us
  Pallas kernels  33 us (76%)
  waiting for transfers between devices  5.03 us (12%)
  starting transfers between devices  4.58 us (11%)
  between operations  0.66 us (2%)
    pallas_call x1, Pallas kernels, shards(): pl.pallas_call(main_kernel, out_shape=(jax.ShapeDtypeStruct((tokens, chan...  28.8 us
    ppermute x1, waiting for transfers between devices, shards(): second_side = lax.ppermute(payload, RING, far)  5.02 us
    ppermute x1, starting transfers between devices, shards(): second_side = lax.ppermute(payload, RING, far)  4.51 us
    pallas_call x1, Pallas kernels, shards(): pl.pallas_call(project_kernel, out_shape=jax.ShapeDtypeStruct((payload_ro...  4.19 us
  transfers between devices with their start and end apart: 2, of which 1 were waited for; matrix products, arithmetic and copies ran while one was open for 0% of the time, Pallas kernels for 0%

profile of v3, /device:TPU:1, one launch (start us, length us, event | category | flops | bytes accessed | tf_op | source)
XLA Modules:
  0.0 43.3 jit_solution(7823869682571366968)
XLA Ops:
  0.6 4.2 %project.1.own_hbm = bf16[784,128]{1,0:T(8,128)(2,1)} custom-call(bf16[3072,128]{1,0:T(8,128)(2,1)} %bitcast.4, bf16[16,128]{1,0:T(8,128)(2,1)} %bitcast.6, bf16[384,128]{1,0:T(8,128)(2,1)} %atom_hbm.1, s32[384]{0:T(512)} %token_hbm.1, s32[48]{0:T(128)} %atoms_of_hbm.1, s32[12]{0:T(128)} %offset_hbm.1), custom_call_target="tpu_custom_call" | custom-call | tf_op jit(solution)/shard_map/project/pallas_call | solution.py:563
  4.8 4.5 %collective-permute-start.1 = (bf16[784,128]{1,0:T(8,128)(2,1)}, bf16[784,128]{1,0:T(8,128)(2,1)S(1)}, u32[]{:S(2)}, u32[]{:S(2)}) collective-permute-start(bf16[784,128]{1,0:T(8,128)(2,1)} %project.1.own_hbm), channel_id=1, source_target_pairs={{1,2},{2,1},{3,4},{4,3},{5,6},{6,5},{7,8},{8,7},{9,10},{10,9},{11,... | collective-permute-start | bytes 602120 | tf_op jit(solution)/shard_map/ppermute | solution.py:592
  9.3 0.1 collective-permute-start
  9.4 5.0 %collective-permute-done.1.far_hbm = bf16[784,128]{1,0:T(8,128)(2,1)S(1)} collective-permute-done((bf16[784,128]{1,0:T(8,128)(2,1)}, bf16[784,128]{1,0:T(8,128)(2,1)S(1)}, u32[]{:S(2)}, u32[]{:S(2)}) %collective-permute-start.1) | collective-permute-done | bytes 200736 | tf_op jit(solution)/shard_map/ppermute | solution.py:592
  14.4 0.0 collective-permute-done.near_hbm
  14.4 28.8 %encode.1 = (bf16[48,768]{1,0:T(8,128)(2,1)}, bf16[384,128]{1,0:T(8,128)(2,1)}) custom-call(bf16[784,128]{1,0:T(8,128)(2,1)} %project.1.own_hbm, bf16[784,128]{1,0:T(8,128)(2,1)S(1)} %collective-permute-done.near_hbm, bf16[784,128]{1,0:T(8,128)(2,1)S(1)} %collective-permute-done.1.far_hbm, bf16[2,16,128]{2,1,0:T(8,128)(2,1)} %bitcast.5, ...), custom_call_target="tpu_custom_call" | custom-call | tf_op jit(solution)/shard_map/encode/pallas_call | solution.py:609
Async XLA Ops:
  4.8 9.6 %collective-permute-start.1 = (bf16[784,128]{1,0:T(8,128)(2,1)}, bf16[784,128]{1,0:T(8,128)(2,1)S(1)}, u32[]{:S(2)}, u32[]{:S(2)}) collective-permute-start(bf16[784,128]{1,0:T(8,128)(2,1)} %project.1.own_hbm), channel_id=1, source_target_pairs={{1,2},{2,1},{3,4},{4,3},{5,6},{6,5},{7,8},{8,7},{9,10},{10,9},{11,... | collective-permute-start | bytes 602120 | tf_op jit(solution)/shard_map/ppermute | solution.py:592
  9.3 5.1 %collective-permute-start = (bf16[784,128]{1,0:T(8,128)(2,1)}, bf16[784,128]{1,0:T(8,128)(2,1)S(1)}, u32[]{:S(2)}, u32[]{:S(2)}) collective-permute-start(bf16[784,128]{1,0:T(8,128)(2,1)} %project.1.own_hbm), channel_id=1, source_target_pairs={{0,1},{1,0},{2,3},{3,2},{4,5},{5,4},{6,7},{7,6},{8,9},{9,8},{10,11... | collective-permute-start | bytes 602120 | tf_op jit(solution)/shard_map/ppermute | solution.py:591

commit v4 on v3

--- a/solution.py
+++ b/solution.py
@@ -493,7 +493,7 @@
             hidden = (gate_part / (1.0 + jnp.exp(-gate_part)) * up_part).astype(BF16)
             act_ref[where, :] = act + dot(hidden, w_trans_out_ref[layer])
 
-    chunk_of = (288, 336, 240)
+    chunk_of = (864, 672, 480)
     for layer in range(BLOCKS):
         first_window = layer * HALO // QB
         last_window = window_count - layer * HALO // QB
@@ -509,7 +509,8 @@
                 attend(layer, first_window + step * (windows // 3) + w)
             return carry
 
-        lax.fori_loop(0, 3, attend_step, 0)
+        for step in range(3):
+            attend_step(step, 0)
         dense(layer, query_first, query_rows, chunk_of[layer])
 
     atom_out_ref[...] = act_ref[atoms : 2 * atoms, :].astype(BF16)

time: 43.5 us -> 35.2 us (0.81)
  Pallas kernels: 33 us -> 24.7 us
    pallas_call x1, Pallas kernels: 28.8 us -> 20.5 us  [shards(): pl.pallas_call(main_kernel, out_shape=(jax.ShapeDtypeStruct((tokens, chan...]
where the time goes in v4:
time: 35.2 us; the launch traced here: 34.9 us
  Pallas kernels  24.7 us (70%)
  waiting for transfers between devices  5.03 us (14%)
  starting transfers between devices  4.58 us (13%)
  between operations  0.66 us (2%)
    pallas_call x1, Pallas kernels, shards(): pl.pallas_call(main_kernel, out_shape=(jax.ShapeDtypeStruct((tokens, chan...  20.5 us
    ppermute x1, waiting for transfers between devices, shards(): second_side = lax.ppermute(payload, RING, far)  5.02 us
    ppermute x1, starting transfers between devices, shards(): second_side = lax.ppermute(payload, RING, far)  4.51 us
    pallas_call x1, Pallas kernels, shards(): pl.pallas_call(project_kernel, out_shape=jax.ShapeDtypeStruct((payload_ro...  4.19 us
  transfers between devices with their start and end apart: 2, of which 1 were waited for; matrix products, arithmetic and copies ran while one was open for 0% of the time, Pallas kernels for 0%

profile of v4, /device:TPU:1, one launch (start us, length us, event | category | flops | bytes accessed | tf_op | source)
XLA Modules:
  0.0 34.9 jit_solution(452644508586014335)
XLA Ops:
  0.6 4.2 %project.1.own_hbm = bf16[784,128]{1,0:T(8,128)(2,1)} custom-call(bf16[3072,128]{1,0:T(8,128)(2,1)} %bitcast.4, bf16[16,128]{1,0:T(8,128)(2,1)} %bitcast.6, bf16[384,128]{1,0:T(8,128)(2,1)} %atom_hbm.1, s32[384]{0:T(512)} %token_hbm.1, s32[48]{0:T(128)} %atoms_of_hbm.1, s32[12]{0:T(128)} %offset_hbm.1), custom_call_target="tpu_custom_call" | custom-call | tf_op jit(solution)/shard_map/project/pallas_call | solution.py:564
  4.8 4.5 %collective-permute-start.1 = (bf16[784,128]{1,0:T(8,128)(2,1)}, bf16[784,128]{1,0:T(8,128)(2,1)S(1)}, u32[]{:S(2)}, u32[]{:S(2)}) collective-permute-start(bf16[784,128]{1,0:T(8,128)(2,1)} %project.1.own_hbm), channel_id=1, source_target_pairs={{1,2},{2,1},{3,4},{4,3},{5,6},{6,5},{7,8},{8,7},{9,10},{10,9},{11,... | collective-permute-start | bytes 602120 | tf_op jit(solution)/shard_map/ppermute | solution.py:593
  9.3 0.1 collective-permute-start
  9.4 5.0 %collective-permute-done.1.far_hbm = bf16[784,128]{1,0:T(8,128)(2,1)S(1)} collective-permute-done((bf16[784,128]{1,0:T(8,128)(2,1)}, bf16[784,128]{1,0:T(8,128)(2,1)S(1)}, u32[]{:S(2)}, u32[]{:S(2)}) %collective-permute-start.1) | collective-permute-done | bytes 200736 | tf_op jit(solution)/shard_map/ppermute | solution.py:593
  14.4 0.0 collective-permute-done.near_hbm
  14.4 20.5 %encode.1 = (bf16[48,768]{1,0:T(8,128)(2,1)}, bf16[384,128]{1,0:T(8,128)(2,1)}) custom-call(bf16[784,128]{1,0:T(8,128)(2,1)} %project.1.own_hbm, bf16[784,128]{1,0:T(8,128)(2,1)S(1)} %collective-permute-done.near_hbm, bf16[784,128]{1,0:T(8,128)(2,1)S(1)} %collective-permute-done.1.far_hbm, bf16[2,16,128]{2,1,0:T(8,128)(2,1)} %bitcast.5, ...), custom_call_target="tpu_custom_call" | custom-call | tf_op jit(solution)/shard_map/encode/pallas_call | solution.py:610
Async XLA Ops:
  4.8 9.6 %collective-permute-start.1 = (bf16[784,128]{1,0:T(8,128)(2,1)}, bf16[784,128]{1,0:T(8,128)(2,1)S(1)}, u32[]{:S(2)}, u32[]{:S(2)}) collective-permute-start(bf16[784,128]{1,0:T(8,128)(2,1)} %project.1.own_hbm), channel_id=1, source_target_pairs={{1,2},{2,1},{3,4},{4,3},{5,6},{6,5},{7,8},{8,7},{9,10},{10,9},{11,... | collective-permute-start | bytes 602120 | tf_op jit(solution)/shard_map/ppermute | solution.py:593
  9.3 5.1 %collective-permute-start = (bf16[784,128]{1,0:T(8,128)(2,1)}, bf16[784,128]{1,0:T(8,128)(2,1)S(1)}, u32[]{:S(2)}, u32[]{:S(2)}) collective-permute-start(bf16[784,128]{1,0:T(8,128)(2,1)} %project.1.own_hbm), channel_id=1, source_target_pairs={{0,1},{1,0},{2,3},{3,2},{4,5},{5,4},{6,7},{7,6},{8,9},{9,8},{10,11... | collective-permute-start | bytes 602120 | tf_op jit(solution)/shard_map/ppermute | solution.py:592

commit v5 on v4

v5 whole, which is shorter than its diff:
```python
import math

import jax
import jax.numpy as jnp
from jax import lax
from jax.experimental import pallas as pl
from jax.experimental.pallas import tpu as pltpu
from jax.sharding import PartitionSpec as P

BLOCKS = 3
QB = 32
KW = 128
HALO = 96
LANES = 128
PAIR_DEPTH = 4
PAIR_SLOTS = 4
PAIR_GROUP = 3
GROUP_BITS = 4
EARLY = 15
EPSILON = 1e-05
RING = ("seq", "chan", "sub")
NT = (((1,), (1,)), ((), ()))
F32 = jnp.float32
BF16 = jnp.bfloat16


def dot(a, b):
    return jnp.dot(a, b, preferred_element_type=F32)


def dot_nt(a, b):
    return lax.dot_general(a, b, NT, preferred_element_type=F32)


def iota(shape, axis):
    return lax.broadcasted_iota(jnp.int32, shape, axis)


def shard_place():
    index, count = 0, 1
    for name in RING:
        index = index * lax.axis_size(name) + lax.axis_index(name)
        count = count * lax.axis_size(name)
    return index, count


def normalize(values, axis):
    centre = jnp.mean(values, axis=axis, keepdims=True)
    shifted = values - centre
    spread = jnp.mean(shifted * shifted, axis=axis, keepdims=True)
    return shifted * lax.rsqrt(spread + EPSILON)


def project_kernel(
    pair_hbm,
    wz_hbm,
    atom_hbm,
    token_hbm,
    atoms_of_hbm,
    offset_hbm,
    out_hbm,
    pair_ref,
    wz_ref,
    token_ref,
    atoms_of_ref,
    offset_ref,
    band_ref,
    meta_ref,
    small_sems,
    in_sems,
    out_sems,
):
    rows, width = pair_ref.shape
    atoms = atom_hbm.shape[0]
    tokens = atoms_of_hbm.shape[0]
    channels = wz_hbm.shape[0]
    tiles = atoms // LANES
    parts = in_sems.shape[0]
    step = rows // parts
    band_step = channels * step // LANES
    meta = atoms + channels * rows // LANES

    loads = [
        pltpu.make_async_copy(
            pair_hbm.at[pl.ds(step * part, step)],
            pair_ref.at[pl.ds(step * part, step)],
            in_sems.at[part],
        )
        for part in range(parts)
    ]
    small = [
        pltpu.make_async_copy(wz_hbm, wz_ref, small_sems.at[0]),
        pltpu.make_async_copy(token_hbm, token_ref, small_sems.at[1]),
        pltpu.make_async_copy(atoms_of_hbm, atoms_of_ref, small_sems.at[2]),
        pltpu.make_async_copy(offset_hbm, offset_ref, small_sems.at[3]),
    ]
    atom_copy = pltpu.make_async_copy(atom_hbm, out_hbm.at[pl.ds(0, atoms)], out_sems.at[parts])
    loads[0].start()
    for copy in small + loads[1:]:
        copy.start()
    atom_copy.start()

    eye = iota((width, width), 0) == iota((width, width), 1)
    centring = (eye.astype(F32) - 1.0 / width).astype(BF16)
    average = jnp.full((channels, width), 1.0 / width, BF16)
    for copy in small:
        copy.wait()
    index, _ = shard_place()
    meta_ref[...] = jnp.zeros_like(meta_ref)
    base = (index - 1) * tokens
    for tile in range(tiles):
        local = token_ref[LANES * tile : LANES * (tile + 1)].reshape(1, LANES) - base
        meta_ref[tile : tile + 1, :] = local.astype(F32)
    meta_ref[tiles : tiles + 1, 0 : offset_ref.shape[0]] = (
        offset_ref[...].reshape(1, offset_ref.shape[0]).astype(F32)
    )
    meta_ref[tiles + 1 : tiles + 2, 0:tokens] = (
        atoms_of_ref[...].reshape(1, tokens).astype(F32)
    )
    band_ref[meta - atoms :, :] = meta_ref[...].astype(BF16)
    stores = []
    for part in range(parts):
        loads[part].wait()
        shifted = dot(pair_ref[step * part : step * (part + 1), :], centring)
        spread = dot_nt(average, (shifted * shifted).astype(BF16))
        projected = dot_nt(wz_ref[...], shifted.astype(BF16))
        projected = (projected * lax.rsqrt(spread + EPSILON)).astype(BF16)
        for tile in range(step // LANES):
            row = band_step * part + channels * tile
            band_ref[row : row + channels, :] = projected[:, LANES * tile : LANES * (tile + 1)]
        first, count = band_step * part, band_step + (16 if part == parts - 1 else 0)
        copy = pltpu.make_async_copy(
            band_ref.at[pl.ds(first, count)],
            out_hbm.at[pl.ds(atoms + first, count)],
            out_sems.at[part],
        )
        copy.start()
        stores.append(copy)
    for copy in stores:
        copy.wait()
    atom_copy.wait()


class Refs:
    def __init__(self, names, refs):
        self.__dict__.update(zip(names, refs))


PAIR_NAMES = (
    "payload_ref",
    "w_single_ref",
    "w_mlp_ref",
    "w_bias_ref",
    "scalars_vmem",
    "scalars",
    "token_rows",
    "key_terms",
    "token_shift",
    "token_base",
    "table_rows",
    "band_ref",
    "side_ref",
    "column_ref",
    "start_ref",
    "second_ref",
    "third_ref",
    "normed_ref",
    "left_terms",
    "right_terms",
    "mlp_ref",
    "bias_weight_ref",
    "act_ref",
    "held_ref",
    "sems",
)
MAIN_NAMES = (
    "w_attn_ref",
    "w_out_ref",
    "w_in_ref",
    "w_trans_out_ref",
    "w_token_ref",
    "bias_ref",
    "query_ref",
    "gate_ref",
    "key_ref",
    "value_ref",
    "gated_ref",
    "feature_ref",
    "weight_sems",
)


def key_start(r, n):
    offset_lanes = r.act_ref.shape[0] // 3 // QB
    return HALO + QB * n + r.scalars[0, n + offset_lanes - 2 * HALO // QB]


def pair_windows(r, own_hbm, near_hbm, far_hbm, small_hbm, first_window, groups, bias_at):
    index, count = shard_place()
    channels = r.w_mlp_ref.shape[1]
    heads = r.w_bias_ref.shape[1]
    width = r.act_ref.shape[1]
    atoms = r.act_ref.shape[0] // 3
    tokens = r.table_rows.shape[0] * 2 // (3 * channels)
    tiles = atoms // LANES
    pairs = tokens // 2
    meta = atoms + channels * pairs
    first_valid = jnp.where(index == 0, atoms, 0)
    end_valid = jnp.where(index == count - 1, 2 * atoms, 3 * atoms)
    first_query = 2 * HALO
    even = index % 2 == 0
    copies = [
        pltpu.make_async_copy(own_hbm, r.payload_ref.at[1], r.sems.at[0]),
        pltpu.make_async_copy(near_hbm, r.payload_ref.at[jnp.where(even, 2, 0)], r.sems.at[1]),
    ]
    if far_hbm is not None:
        copies.append(
            pltpu.make_async_copy(far_hbm, r.payload_ref.at[jnp.where(even, 0, 2)], r.sems.at[2])
        )
    small_copies = [
        pltpu.make_async_copy(source, target, r.sems.at[3 + i])
        for i, (source, target) in enumerate(
            zip(small_hbm, (r.w_single_ref, r.w_mlp_ref, r.w_bias_ref))
        )
    ]
    for copy in small_copies + copies:
        copy.start()
    for copy in small_copies:
        copy.wait()

    big = 256
    group = 1 << GROUP_BITS
    select = (iota((big, channels), 0) >> GROUP_BITS == iota((big, channels), 1)).astype(BF16)
    same_query = ((iota((big, big), 0) ^ iota((big, big), 1)) & (group - 1)) == 0
    for layer in range(3):
        by_row = dot_nt(select, r.w_mlp_ref[layer]).astype(BF16)
        r.mlp_ref[layer] = jnp.where(same_query, dot_nt(by_row, select), 0.0).astype(BF16)
    per_block = heads * group
    pick_head = (iota((per_block, heads), 0) >> GROUP_BITS == iota((per_block, heads), 1)).astype(BF16)
    for layer in range(BLOCKS):
        by_row = dot(pick_head, r.w_bias_ref[layer]).astype(BF16)
        r.bias_weight_ref[layer * per_block : (layer + 1) * per_block, :] = jnp.where(
            same_query[0:per_block], dot_nt(by_row, select), 0.0
        ).astype(BF16)

    for copy in copies:
        copy.wait()
    if far_hbm is None:
        absent = jnp.where(even, 0, 2)
        r.payload_ref[absent] = jnp.zeros_like(r.payload_ref[absent])
    sides = tuple(r.payload_ref.at[side] for side in range(3))
    metas = [ref[meta : meta + 16, :].astype(F32) for ref in sides]
    number = iota((3 * tiles, LANES), 0) * LANES + iota((3 * tiles, LANES), 1)
    relative = jnp.concatenate(
        [m[0:tiles] + s for m, s in zip(metas, (-tokens, 0, tokens))], axis=0
    )
    inside = (number >= first_valid) & (number < end_valid)
    relative = jnp.where(inside, relative, -64.0)
    relative_int = relative.astype(jnp.int32)
    offset_lanes = atoms // QB
    offset_row = (
        metas[0][3:4]
        + pltpu.roll(metas[1][3:4], offset_lanes, 1)
        + pltpu.roll(metas[2][3:4], 2 * offset_lanes, 1)
    )
    r.scalars_vmem[...] = jnp.broadcast_to(offset_row, (8, LANES)).astype(jnp.int32)
    copy = pltpu.make_async_copy(r.scalars_vmem, r.scalars, r.sems.at[6])
    copy.start()
    for tile in range(3 * tiles):
        r.token_rows[tile] = jnp.broadcast_to(relative_int[tile : tile + 1], (8, LANES))
    r.token_rows[3 * tiles] = jnp.zeros((8, LANES), jnp.int32)

    eye = iota((LANES, LANES), 0) == iota((LANES, LANES), 1)
    ones = jnp.ones((LANES, LANES), BF16)
    for side, ref in enumerate(sides):
        for tile in range(tiles):
            rows = ref[tile * LANES : (tile + 1) * LANES, :]
            at = side * tiles + tile
            where = slice(at * LANES, (at + 1) * LANES)
            r.act_ref[where, :] = rows.astype(F32)
            r.held_ref[where, :] = (
                (iota((LANES, LANES), 0) + at * LANES >= first_valid)
                & (iota((LANES, LANES), 0) + at * LANES < end_valid)
            ).astype(F32)
            relu = jnp.maximum(rows, jnp.zeros((), BF16))
            r.key_terms[at] = dot_nt(r.w_single_ref[1], relu).astype(BF16).astype(F32)
            column = dot(jnp.where(eye, relative[at : at + 1], 0.0).astype(BF16), ones)
            column = column.astype(jnp.int32)
            base = (column & 1) * (LANES // 2)
            r.token_base[where, :] = base
            r.token_shift[where, :] = LANES // 4 - column
        for pair in range(pairs):
            row = atoms + channels * pair
            to = (side * pairs + pair) * channels
            r.table_rows[to : to + channels, :] = ref[row : row + channels, :].astype(F32)
    r.key_terms[3 * tiles] = jnp.zeros((channels, LANES), F32)

    w_query = jnp.transpose(r.w_single_ref[0].astype(F32))
    window_rows = QB * PAIR_GROUP * groups
    first_row = pl.multiple_of(first_query + QB * first_window, QB)
    for row in range(0, window_rows, QB * PAIR_GROUP):
        where = pl.ds(pl.multiple_of(first_row + row, QB), QB * PAIR_GROUP)
        token = LANES // 4 - r.token_shift[where, :]
        hit = ((token >> 1) == iota(token.shape, 1)).astype(F32).astype(BF16)
        r.left_terms[where, 0:LANES] = hit
        r.left_terms[where, LANES:] = jnp.maximum(r.act_ref[where, :], 0.0).astype(BF16)
    padded = -(-3 * pairs // 16) * 16
    for c in range(channels):
        at = slice(c % 2 * LANES, (c % 2 + 1) * LANES)
        rows = [
            r.table_rows[pl.ds(8 * channels * g + c, 8, stride=channels), :]
            for g in range(3 * pairs // 8)
        ]
        rows.append(jnp.zeros((padded - 3 * pairs, LANES), F32))
        r.right_terms[c // 2, 0:padded, at] = jnp.concatenate(rows, axis=0).astype(BF16)
        r.right_terms[c // 2, padded:LANES, at] = jnp.zeros((LANES - padded, LANES), BF16)
        r.right_terms[c // 2, LANES:, at] = jnp.broadcast_to(
            w_query[:, c : c + 1], (width, LANES)
        ).astype(BF16)

    for c in range(channels // 2):
        band = dot(r.left_terms[pl.ds(first_row, window_rows), :], r.right_terms[c])
        for d in range(2):
            at = slice(d * LANES, (d + 1) * LANES)
            r.band_ref[2 * c + d, pl.ds(first_row, window_rows), :] = band[:, at]

    copy.wait()
    lane = iota((channels, LANES), 1)
    lane8 = iota((8, LANES), 1)
    log2e = math.log2(math.e)

    def window_at(step, w):
        return first_window + step * PAIR_GROUP + w

    def column_stage(step, w):
        n = window_at(step, w)
        query = pl.multiple_of(first_query + QB * n, QB)
        start = key_start(r, n)
        tile = start // LANES
        shift = start % LANES
        back = LANES - shift
        key_tokens = pltpu.roll(
            jnp.where(lane8 >= shift, r.token_rows[tile], r.token_rows[tile + 1]), back, 1
        )
        r.side_ref[w] = pltpu.roll(
            jnp.where(lane >= shift, r.key_terms[tile], r.key_terms[tile + 1]), back, 1
        )
        for g in range(QB // 8):
            rows = pl.ds(query + 8 * g, 8)
            r.column_ref[w, 8 * g : 8 * g + 8, :] = (
                jnp.clip(key_tokens + r.token_shift[rows, :], 0, LANES // 2 - 1)
                + r.token_base[rows, :]
            )

    def start_stage(step, w):
        query = pl.multiple_of(first_query + QB * window_at(step, w), QB)
        slot = step % PAIR_SLOTS
        for g in range(QB // 8):
            half, part = g // (group // 8), g % (group // 8)
            at = slice(half * LANES, (half + 1) * LANES)
            column = r.column_ref[w, 8 * g : 8 * g + 8, :]
            rows = pl.ds(query + 8 * g, 8)
            for e in range(channels):
                row = e * group + 8 * part
                r.start_ref[slot, w, row : row + 8, at] = jnp.take_along_axis(
                    r.band_ref[e, rows, :], column, axis=1, mode="promise_in_bounds"
                ) + jnp.broadcast_to(r.side_ref[w, e : e + 1, :], (8, LANES))

    def relu(values):
        return jnp.maximum(values.astype(BF16), jnp.zeros((), BF16))

    def first_stage(step, w):
        slot = (step + 3) % PAIR_SLOTS
        r.second_ref[w] = relu(dot(r.mlp_ref[0], relu(r.start_ref[slot, w])))

    def second_stage(w):
        r.third_ref[w] = relu(dot(r.mlp_ref[1], r.second_ref[w]))

    def norm_stage(step, w):
        slot = (step + 1) % PAIR_SLOTS
        third = dot(r.mlp_ref[2], r.third_ref[w])
        for half in range(2):
            at = slice(half * LANES, (half + 1) * LANES)
            normed = []
            for part in range(group // 8):
                pair = [
                    third[e * group + 8 * part : e * group + 8 * part + 8, at]
                    + r.start_ref[slot, w, e * group + 8 * part : e * group + 8 * part + 8, at]
                    for e in range(channels)
                ]
                centre = sum(pair[1:], pair[0]) * (1.0 / channels)
                shifted = [p - centre for p in pair]
                spread = sum([s * s for s in shifted[1:]], shifted[0] * shifted[0])
                factor = lax.rsqrt(spread * (1.0 / channels) + EPSILON) * log2e
                normed.append([s * factor for s in shifted])
            for e in range(channels):
                rows = jnp.concatenate([n[e] for n in normed], axis=0)
                r.normed_ref[w, e * group : (e + 1) * group, at] = rows.astype(BF16)

    def bias_stage(step, w):
        to_ref = bias_at((step - PAIR_DEPTH) * PAIR_GROUP + w)
        bias = dot(r.bias_weight_ref[...], r.normed_ref[w])
        for layer in range(BLOCKS):
            part = bias[layer * per_block : (layer + 1) * per_block]
            to_ref[layer, 0:per_block, :] = part[:, 0:LANES]
            to_ref[layer, per_block : 2 * per_block, :] = part[:, LANES:]

    def pair_step(step, carry=None):
        def live(behind):
            return not isinstance(step, int) or 0 <= step - behind < groups

        for w in range(PAIR_GROUP):
            if live(4):
                bias_stage(step, w)
            if live(3):
                norm_stage(step, w)
            if live(2):
                second_stage(w)
            if live(1):
                first_stage(step, w)
            if live(0):
                column_stage(step, w)
                start_stage(step, w)
        return carry

    for step in range(PAIR_DEPTH):
        pair_step(step)
    if groups > PAIR_DEPTH:
        lax.fori_loop(PAIR_DEPTH, groups + jnp.minimum(index, 0), pair_step, 0)
    for step in range(max(groups, PAIR_DEPTH), groups + PAIR_DEPTH):
        pair_step(step)
    return metas, relative_int


def window_split(window_count):
    early = EARLY
    even = lax.rem(shard_place()[0], 2) == 0
    return early, jnp.where(even, window_count - early, 0), jnp.where(even, 0, early)


def early_kernel(own_hbm, near_hbm, w_single_hbm, w_mlp_hbm, w_bias_hbm, out_ref, *scratch):
    r = Refs(PAIR_NAMES, scratch)
    atoms = r.act_ref.shape[0] // 3
    early, first_window, _ = window_split((atoms + 5 * HALO) // QB)
    pair_windows(
        r,
        own_hbm,
        near_hbm,
        None,
        (w_single_hbm, w_mlp_hbm, w_bias_hbm),
        first_window,
        early // PAIR_GROUP,
        lambda n: out_ref.at[n],
    )


def main_kernel(
    own_hbm,
    near_hbm,
    far_hbm,
    early_ref,
    w_single_hbm,
    w_mlp_hbm,
    w_bias_hbm,
    w_attn_hbm,
    w_out_hbm,
    w_in_hbm,
    w_trans_out_hbm,
    w_token_hbm,
    token_out_ref,
    atom_out_ref,
    *scratch,
):
    r = Refs(PAIR_NAMES + MAIN_NAMES, scratch)
    index, count = shard_place()
    atoms, width = atom_out_ref.shape
    tokens = token_out_ref.shape[0]
    heads = r.w_bias_ref.shape[1]
    head_size = width // heads
    tiles = atoms // LANES
    group = QB // 2
    per_block = heads * group
    log2e = math.log2(math.e)
    first_query = 2 * HALO
    window_count = (atoms + 5 * HALO) // QB
    early, early_first, late_first = window_split(window_count)
    even = lax.rem(index, 2) == 0
    weight_copies = [
        pltpu.make_async_copy(source, target, r.weight_sems.at[i])
        for i, (source, target) in enumerate(
            (
                (w_attn_hbm, r.w_attn_ref),
                (w_out_hbm, r.w_out_ref),
                (w_in_hbm, r.w_in_ref),
                (w_trans_out_hbm, r.w_trans_out_ref),
                (w_token_hbm, r.w_token_ref),
            )
        )
    ]
    for copy in weight_copies:
        copy.start()
    metas, relative_int = pair_windows(
        r,
        own_hbm,
        near_hbm,
        far_hbm,
        (w_single_hbm, w_mlp_hbm, w_bias_hbm),
        late_first,
        (window_count - early) // PAIR_GROUP,
        lambda n: r.bias_ref.at[n],
    )
    for copy in weight_copies:
        copy.wait()
    head_of_lane = iota((QB // 2, width), 1) // head_size
    scale = log2e / math.sqrt(head_size)

    def project(layer, first, rows, chunk):
        w_first = jnp.concatenate([r.w_attn_ref[layer, 0], r.w_attn_ref[layer, 1]], axis=1)
        w_second = jnp.concatenate([r.w_attn_ref[layer, 2], r.w_attn_ref[layer, 3]], axis=1)
        for row in range(first, first + rows, chunk):
            where = slice(row, row + chunk)
            normed = normalize(r.act_ref[where, :], 1).astype(BF16)
            held = r.held_ref[where, :] > 0.0
            both = dot(normed, w_first)
            r.query_ref[where, :] = (both[:, :width] * scale).astype(BF16)
            r.key_ref[where, :] = jnp.where(held, both[:, width:], 0.0)
            both = dot(normed, w_second)
            r.value_ref[where, :] = jnp.where(held, both[:, :width], 0.0)
            r.gate_ref[where, :] = jax.nn.sigmoid(both[:, width:])

    def attend(layer, n, bias):
        query = pl.multiple_of(first_query + QB * n, QB)
        start = key_start(r, n)
        q = r.query_ref[pl.ds(query, QB), :]
        k = r.key_ref[pl.ds(start, KW), :].astype(BF16)
        v = jnp.concatenate(
            [r.value_ref[pl.ds(start, KW), :], r.held_ref[pl.ds(start, KW), :]], axis=1
        ).astype(BF16)
        blocks = []
        for half in range(2):
            part = q[half * QB // 2 : (half + 1) * QB // 2]
            for h in range(heads):
                blocks.append(jnp.where(head_of_lane == h, part, jnp.zeros((), BF16)))
        scores = dot_nt(jnp.concatenate(blocks, axis=0), k) + bias
        sums = dot(jnp.exp2(scores).astype(BF16), v)
        halves = []
        for half in range(2):
            base = half * per_block
            value = sums[base : base + group, :LANES]
            total = sums[base : base + group, LANES:]
            for h in range(1, heads):
                row = base + h * group
                value = jnp.where(head_of_lane == h, sums[row : row + group, :LANES], value)
                total = jnp.where(head_of_lane == h, sums[row : row + group, LANES:], total)
            halves.append(value / total)
        attended = jnp.concatenate(halves, axis=0)
        r.gated_ref[pl.ds(query, QB), :] = (attended * r.gate_ref[pl.ds(query, QB), :]).astype(BF16)

    def dense(layer, first, rows, chunk):
        for row in range(first, first + rows, chunk):
            where = slice(row, row + chunk)
            act = r.act_ref[where, :] + dot(r.gated_ref[where, :], r.w_out_ref[layer])
            act = jnp.where(r.held_ref[where, :] > 0.0, act, 0.0)
            normed = normalize(act, 1).astype(BF16)
            gate_part = dot(normed, r.w_in_ref[layer, 0])
            up_part = dot(normed, r.w_in_ref[layer, 1])
            hidden = (gate_part / (1.0 + jnp.exp(-gate_part)) * up_part).astype(BF16)
            r.act_ref[where, :] = act + dot(hidden, r.w_trans_out_ref[layer])

    chunk_of = (864, 672, 480)
    for layer in range(BLOCKS):
        first_window = layer * HALO // QB
        last_window = window_count - layer * HALO // QB
        windows = last_window - first_window
        query_first = first_query + QB * first_window
        query_rows = QB * windows
        key_first = query_first - HALO
        key_rows = query_rows + 2 * HALO
        project(layer, key_first, key_rows, key_rows // 3)

        skipped = layer * HALO // QB
        from_early = jnp.where(even, 0, skipped)
        from_late = jnp.where(even, skipped, 0)
        for w in range(early - skipped):
            n = from_early + w
            attend(layer, early_first + n, early_ref[n, layer])
        for w in range(window_count - early - skipped):
            n = from_late + w
            attend(layer, late_first + n, r.bias_ref[n, layer])
        dense(layer, query_first, query_rows, chunk_of[layer])

    atom_out_ref[...] = r.act_ref[atoms : 2 * atoms, :].astype(BF16)
    reach = atoms + LANES
    r.feature_ref[atoms + HALO : reach, :] = jnp.zeros_like(r.feature_ref[atoms + HALO : reach, :])
    for row in range(0, atoms + HALO, 160):
        rows = r.act_ref[atoms + row : atoms + row + 160, :].astype(BF16)
        features = jnp.maximum(dot(rows, r.w_token_ref[...]), 0.0)
        r.feature_ref[row : row + 160, :] = features.astype(BF16)
    slot = iota((tokens, LANES), 0) + tokens
    member = jnp.concatenate(
        [
            (slot == relative_int[tile : tile + 1]).astype(F32)
            for tile in range(tiles, 2 * tiles + 1)
        ],
        axis=1,
    ).astype(BF16)
    sums = dot(member, r.feature_ref[...])
    diagonal = (iota((tokens, LANES), 0) == iota((tokens, LANES), 1)).astype(F32)
    atoms_of = jnp.sum(diagonal * metas[1][4:5], axis=1, keepdims=True)
    token_out_ref[...] = (sums / atoms_of).astype(BF16)


def shards(
    atom_single,
    atom_token,
    token_atoms,
    window_offset,
    token_pair,
    w_zpair,
    w_single,
    w_pair_mlp,
    w_bias,
    w_attn,
    w_out,
    w_trans_in,
    w_trans_out,
    w_token,
):
    index, count = shard_place()
    atoms, width = atom_single.shape
    tokens, band, depth = token_pair.shape
    channels = w_zpair.shape[1]
    tiles = atoms // LANES
    pairs = tokens * band // LANES
    payload_rows = atoms + channels * pairs + 16

    vmem = pl.BlockSpec(memory_space=pltpu.VMEM)
    anywhere = pl.BlockSpec(memory_space=pl.ANY)
    parts = 3
    payload = pl.pallas_call(
        project_kernel,
        out_shape=jax.ShapeDtypeStruct((payload_rows, width), BF16),
        in_specs=[anywhere] * 6,
        out_specs=anywhere,
        scratch_shapes=[
            pltpu.VMEM((tokens * band, depth), BF16),
            pltpu.VMEM((channels, depth), BF16),
            pltpu.VMEM((atoms,), jnp.int32),
            pltpu.VMEM((tokens,), jnp.int32),
            pltpu.VMEM(window_offset.shape, jnp.int32),
            pltpu.VMEM((payload_rows - atoms, width), BF16),
            pltpu.VMEM((16, width), F32),
            pltpu.SemaphoreType.DMA((4,)),
            pltpu.SemaphoreType.DMA((parts,)),
            pltpu.SemaphoreType.DMA((parts + 1,)),
        ],
        name="project",
    )(
        token_pair.reshape(tokens * band, depth),
        jnp.swapaxes(w_zpair, 0, 1),
        atom_single,
        atom_token,
        token_atoms,
        window_offset,
    )
    near = [(i, i ^ 1) for i in range(count)]
    far = [(i, ((i + 1) ^ 1) - 1) for i in range(1, count - 1)]
    first_side = lax.ppermute(payload, RING, near)
    second_side = lax.ppermute(payload, RING, far)

    in_hbm = pl.BlockSpec(memory_space=pltpu.HBM)
    small = (
        jnp.swapaxes(w_single, 1, 2),
        w_pair_mlp,
        jnp.swapaxes(w_bias, 1, 2),
    )
    large = (w_attn, w_out, w_trans_in, w_trans_out, w_token)
    reach = 3 * atoms
    windows = (atoms + 5 * HALO) // QB
    early, _, _ = window_split(windows)
    heads = w_bias.shape[2]
    channels_out = w_token.shape[1]

    def hbm(*arrays):
        return [pltpu.with_memory_space_constraint(x, pltpu.HBM) for x in arrays]

    pair_scratch = [
        pltpu.VMEM((3, payload_rows, width), BF16),
        *[pltpu.VMEM(w.shape, BF16) for w in small],
        pltpu.VMEM((8, LANES), jnp.int32),
        pltpu.SMEM((8, LANES), jnp.int32),
        pltpu.VMEM((3 * tiles + 1, 8, LANES), jnp.int32),
        pltpu.VMEM((3 * tiles + 1, channels, LANES), F32),
        pltpu.VMEM((reach, LANES), jnp.int32),
        pltpu.VMEM((reach, LANES), jnp.int32),
        pltpu.VMEM((3 * pairs * channels, LANES), F32),
        pltpu.VMEM((channels, reach, LANES), F32),
        pltpu.VMEM((PAIR_GROUP, channels, LANES), F32),
        pltpu.VMEM((PAIR_GROUP, QB, LANES), jnp.int32),
        pltpu.VMEM((PAIR_SLOTS, PAIR_GROUP, 256, 256), F32),
        *[pltpu.VMEM((PAIR_GROUP, 256, 256), BF16)] * 3,
        pltpu.VMEM((reach, 256), BF16),
        pltpu.VMEM((channels // 2, 256, 256), BF16),
        pltpu.VMEM((3, 256, 256), BF16),
        pltpu.VMEM((BLOCKS * heads * 256 // channels, 256), BF16),
        pltpu.VMEM((reach, width), F32),
        pltpu.VMEM((reach, LANES), F32),
        pltpu.SemaphoreType.DMA((7,)),
    ]
    early_bias = pl.pallas_call(
        early_kernel,
        out_shape=jax.ShapeDtypeStruct((early, BLOCKS, heads * QB, KW), F32),
        in_specs=[in_hbm, anywhere] + [in_hbm] * len(small),
        out_specs=vmem,
        scratch_shapes=pair_scratch,
        compiler_params=pltpu.CompilerParams(vmem_limit_bytes=40 * 2**20),
        cost_estimate=pl.CostEstimate(
            flops=2 * 10**9, transcendentals=10**5, bytes_accessed=8 * 10**6
        ),
        name="early_pairs",
    )(*hbm(payload), first_side, *hbm(*small))
    token_single, atom_out = pl.pallas_call(
        main_kernel,
        out_shape=(
            jax.ShapeDtypeStruct((tokens, channels_out), BF16),
            jax.ShapeDtypeStruct((atoms, width), BF16),
        ),
        in_specs=[in_hbm] + [anywhere] * 2 + [vmem] + [in_hbm] * (len(small) + len(large)),
        out_specs=(vmem, vmem),
        scratch_shapes=pair_scratch
        + [
            *[pltpu.VMEM(w.shape, BF16) for w in large],
            pltpu.VMEM((windows - early, BLOCKS, heads * QB, KW), F32),
            pltpu.VMEM((reach, width), BF16),
            pltpu.VMEM((reach, width), F32),
            pltpu.VMEM((reach, width), F32),
            pltpu.VMEM((reach, width), F32),
            pltpu.VMEM((reach, width), BF16),
            pltpu.VMEM((atoms + LANES, channels_out), BF16),
            pltpu.SemaphoreType.DMA((len(large),)),
        ],
        compiler_params=pltpu.CompilerParams(vmem_limit_bytes=48 * 2**20),
        name="encode",
    )(*hbm(payload), first_side, second_side, early_bias, *hbm(*small, *large))
    return token_single, atom_out


def solution(mesh):
    split = ("group", "seq", "chan", "sub")
    in_specs = (
        P(split, None),
        P(split),
        P(split),
        P(split),
        P(split, None, None),
        P(),
        P(),
        P(),
        P(),
        P(),
        P(),
        P(),
        P(),
        P(),
    )
    out_specs = (P(split, None), P(split, None))
    return jax.shard_map(shards, mesh=mesh, in_specs=in_specs, out_specs=out_specs, check_vma=False)
```

time: 35.2 us -> 33.9 us (0.963)
  waiting for transfers between devices: 5.03 us -> 0.01 us
  Pallas kernels: 24.7 us -> 28.2 us
    pallas_call x0 -> x1, Pallas kernels: none -> 7.49 us  [shards(): pl.pallas_call(early_kernel, out_shape=jax.ShapeDtypeStruct((early, BLOCK...]
    ppermute x1, waiting for transfers between devices: 5.02 us -> 0.01 us  [shards(): second_side = lax.ppermute(payload, RING, far)]
    pallas_call x1, Pallas kernels: 20.5 us -> 16.5 us  [shards(): pl.pallas_call(main_kernel, out_shape=(jax.ShapeDtypeStruct((tokens, chan...]
  transfers between devices with their start and end apart: 2 -> 2, of which waited for: 1 -> 0; matrix products, arithmetic and copies ran while one was open for 0% -> 0% of each run, Pallas kernels for 0% -> 22%
where the time goes in v5:
time: 33.9 us; the launch traced here: 33.6 us
  Pallas kernels  28.2 us (83%)
  starting transfers between devices  4.59 us (14%)
  between operations  0.83 us (2%)
    pallas_call x1, Pallas kernels, shards(): pl.pallas_call(main_kernel, out_shape=(jax.ShapeDtypeStruct((tokens, chan...  16.5 us
    pallas_call x1, Pallas kernels, shards(): pl.pallas_call(early_kernel, out_shape=jax.ShapeDtypeStruct((early, BLOCK...  7.49 us
    ppermute x1, starting transfers between devices, shards(): second_side = lax.ppermute(payload, RING, far)  4.46 us
    pallas_call x1, Pallas kernels, shards(): pl.pallas_call(project_kernel, out_shape=jax.ShapeDtypeStruct((payload_ro...  4.19 us
  transfers between devices with their start and end apart: 2, of which 0 were waited for; matrix products, arithmetic and copies ran while one was open for 0% of the time, Pallas kernels for 22%

profile of v5, /device:TPU:1, one launch (start us, length us, event | category | flops | bytes accessed | tf_op | source)
XLA Modules:
  0.0 33.6 jit_solution(10666722766734804480)
XLA Ops:
  0.6 4.2 %project.1.own_hbm = bf16[784,128]{1,0:T(8,128)(2,1)} custom-call(bf16[3072,128]{1,0:T(8,128)(2,1)} %bitcast.4, bf16[16,128]{1,0:T(8,128)(2,1)} %bitcast.7, bf16[384,128]{1,0:T(8,128)(2,1)} %atom_hbm.1, s32[384]{0:T(512)} %token_hbm.1, s32[48]{0:T(128)} %atoms_of_hbm.1, s32[12]{0:T(128)} %offset_hbm.1), custom_call_target="tpu_custom_call" | custom-call | tf_op jit(solution)/shard_map/project/pallas_call | solution.py:640
  4.8 0.1 collective-permute-start
  4.9 4.5 %collective-permute-start.1 = (bf16[784,128]{1,0:T(8,128)(2,1)}, bf16[784,128]{1,0:T(8,128)(2,1)S(1)}, u32[]{:S(2)}, u32[]{:S(2)}) collective-permute-start(bf16[784,128]{1,0:T(8,128)(2,1)} %project.1.own_hbm), channel_id=1, source_target_pairs={{1,2},{2,1},{3,4},{4,3},{5,6},{6,5},{7,8},{8,7},{9,10},{10,9},{11,... | collective-permute-start | bytes 602120 | tf_op jit(solution)/shard_map/ppermute | solution.py:669
  9.4 0.0 collective-permute-done.near_hbm
  9.4 7.5 %early_pairs.1.early_ref = f32[15,3,128,128]{3,2,1,0:T(8,128)S(1)} custom-call(bf16[784,128]{1,0:T(8,128)(2,1)} %project.1.own_hbm, bf16[784,128]{1,0:T(8,128)(2,1)S(1)} %collective-permute-done.near_hbm, bf16[2,16,128]{2,1,0:T(8,128)(2,1)} %bitcast.5, bf16[3,16,16]{2,1,0:T(8,128)(2,1)} %w_mlp_hbm.3, bf16[3,4,16]{2,1,0:T(4,128)(2,1)} %bitcast.8), custom_call_target="tpu_custom_call" | custom-call | flops 2000000000 | bytes 8000000 | tf_op jit(solution)/shard_map/early_pairs/pallas_call | solution.py:710
  16.9 0.0 collective-permute-done.1.far_hbm
  16.9 16.5 %encode.1 = (bf16[48,768]{1,0:T(8,128)(2,1)}, bf16[384,128]{1,0:T(8,128)(2,1)}) custom-call(bf16[784,128]{1,0:T(8,128)(2,1)} %project.1.own_hbm, bf16[784,128]{1,0:T(8,128)(2,1)S(1)} %collective-permute-done.near_hbm, bf16[784,128]{1,0:T(8,128)(2,1)S(1)} %collective-permute-done.1.far_hbm, f32[15,3,128,128]{3,2,1,0:T(8,128)S(1)} %early_pairs.1.early_ref, ...), custom_call_target="tpu_custom_call" | custom-call | tf_op jit(solution)/shard_map/encode/pallas_call | solution.py:722
Async XLA Ops:
  4.8 4.6 %collective-permute-start = (bf16[784,128]{1,0:T(8,128)(2,1)}, bf16[784,128]{1,0:T(8,128)(2,1)S(1)}, u32[]{:S(2)}, u32[]{:S(2)}) collective-permute-start(bf16[784,128]{1,0:T(8,128)(2,1)} %project.1.own_hbm), channel_id=1, source_target_pairs={{0,1},{1,0},{2,3},{3,2},{4,5},{5,4},{6,7},{7,6},{8,9},{9,8},{10,11... | collective-permute-start | bytes 602120 | tf_op jit(solution)/shard_map/ppermute | solution.py:668
  4.9 12.0 %collective-permute-start.1 = (bf16[784,128]{1,0:T(8,128)(2,1)}, bf16[784,128]{1,0:T(8,128)(2,1)S(1)}, u32[]{:S(2)}, u32[]{:S(2)}) collective-permute-start(bf16[784,128]{1,0:T(8,128)(2,1)} %project.1.own_hbm), channel_id=1, source_target_pairs={{1,2},{2,1},{3,4},{4,3},{5,6},{6,5},{7,8},{8,7},{9,10},{10,9},{11,... | collective-permute-start | bytes 602120 | tf_op jit(solution)/shard_map/ppermute | solution.py:669

commit v6 on v5

--- a/solution.py
+++ b/solution.py
@@ -195,7 +195,7 @@
     return HALO + QB * n + r.scalars[0, n + offset_lanes - 2 * HALO // QB]
 
 
-def pair_windows(r, own_hbm, near_hbm, far_hbm, small_hbm, first_window, groups, bias_at):
+def pair_windows(r, own_hbm, near_hbm, far_hbm, small_hbm, first_window, groups, bias_at, later=()):
     index, count = shard_place()
     channels = r.w_mlp_ref.shape[1]
     heads = r.w_bias_ref.shape[1]
@@ -223,7 +223,7 @@
             zip(small_hbm, (r.w_single_ref, r.w_mlp_ref, r.w_bias_ref))
         )
     ]
-    for copy in small_copies + copies:
+    for copy in (*small_copies, *copies, *later):
         copy.start()
     for copy in small_copies:
         copy.wait()
@@ -278,10 +278,11 @@
             at = side * tiles + tile
             where = slice(at * LANES, (at + 1) * LANES)
             r.act_ref[where, :] = rows.astype(F32)
-            r.held_ref[where, :] = (
-                (iota((LANES, LANES), 0) + at * LANES >= first_valid)
-                & (iota((LANES, LANES), 0) + at * LANES < end_valid)
-            ).astype(F32)
+            if far_hbm is not None:
+                r.held_ref[where, :] = (
+                    (iota((LANES, LANES), 0) + at * LANES >= first_valid)
+                    & (iota((LANES, LANES), 0) + at * LANES < end_valid)
+                ).astype(F32)
             relu = jnp.maximum(rows, jnp.zeros((), BF16))
             r.key_terms[at] = dot_nt(r.w_single_ref[1], relu).astype(BF16).astype(F32)
             column = dot(jnp.where(eye, relative[at : at + 1], 0.0).astype(BF16), ones)
@@ -497,8 +498,6 @@
             )
         )
     ]
-    for copy in weight_copies:
-        copy.start()
     metas, relative_int = pair_windows(
         r,
         own_hbm,
@@ -508,6 +507,7 @@
         late_first,
         (window_count - early) // PAIR_GROUP,
         lambda n: r.bias_ref.at[n],
+        weight_copies,
     )
     for copy in weight_copies:
         copy.wait()

time: 33.9 us -> 33.6 us (level)
  Pallas kernels: 28.2 us -> 27.8 us
    pallas_call x1, Pallas kernels: 16.5 us -> 16.2 us  [shards(): pl.pallas_call(main_kernel, out_shape=(jax.ShapeDtypeStruct((tokens, chan...]
where the time goes in v6:
time: 33.6 us; the launch traced here: 33.3 us
  Pallas kernels  27.8 us (83%)
  starting transfers between devices  4.59 us (14%)
  between operations  0.83 us (2%)
    pallas_call x1, Pallas kernels, shards(): pl.pallas_call(main_kernel, out_shape=(jax.ShapeDtypeStruct((tokens, chan...  16.2 us
    pallas_call x1, Pallas kernels, shards(): pl.pallas_call(early_kernel, out_shape=jax.ShapeDtypeStruct((early, BLOCK...  7.49 us
    ppermute x1, starting transfers between devices, shards(): second_side = lax.ppermute(payload, RING, far)  4.46 us
    pallas_call x1, Pallas kernels, shards(): pl.pallas_call(project_kernel, out_shape=jax.ShapeDtypeStruct((payload_ro...  4.19 us
  transfers between devices with their start and end apart: 2, of which 0 were waited for; matrix products, arithmetic and copies ran while one was open for 0% of the time, Pallas kernels for 22%

profile of v6, /device:TPU:1, one launch (start us, length us, event | category | flops | bytes accessed | tf_op | source)
XLA Modules:
  0.0 33.3 jit_solution(1226726822704615442)
XLA Ops:
  0.6 4.2 %project.1.own_hbm = bf16[784,128]{1,0:T(8,128)(2,1)} custom-call(bf16[3072,128]{1,0:T(8,128)(2,1)} %bitcast.4, bf16[16,128]{1,0:T(8,128)(2,1)} %bitcast.7, bf16[384,128]{1,0:T(8,128)(2,1)} %atom_hbm.1, s32[384]{0:T(512)} %token_hbm.1, s32[48]{0:T(128)} %atoms_of_hbm.1, s32[12]{0:T(128)} %offset_hbm.1), custom_call_target="tpu_custom_call" | custom-call | tf_op jit(solution)/shard_map/project/pallas_call | solution.py:640
  4.8 0.1 collective-permute-start
  4.9 4.5 %collective-permute-start.1 = (bf16[784,128]{1,0:T(8,128)(2,1)}, bf16[784,128]{1,0:T(8,128)(2,1)S(1)}, u32[]{:S(2)}, u32[]{:S(2)}) collective-permute-start(bf16[784,128]{1,0:T(8,128)(2,1)} %project.1.own_hbm), channel_id=1, source_target_pairs={{1,2},{2,1},{3,4},{4,3},{5,6},{6,5},{7,8},{8,7},{9,10},{10,9},{11,... | collective-permute-start | bytes 602120 | tf_op jit(solution)/shard_map/ppermute | solution.py:669
  9.4 0.0 collective-permute-done.near_hbm
  9.4 7.5 %early_pairs.1.early_ref = f32[15,3,128,128]{3,2,1,0:T(8,128)S(1)} custom-call(bf16[784,128]{1,0:T(8,128)(2,1)} %project.1.own_hbm, bf16[784,128]{1,0:T(8,128)(2,1)S(1)} %collective-permute-done.near_hbm, bf16[2,16,128]{2,1,0:T(8,128)(2,1)} %bitcast.5, bf16[3,16,16]{2,1,0:T(8,128)(2,1)} %w_mlp_hbm.3, bf16[3,4,16]{2,1,0:T(4,128)(2,1)} %bitcast.8), custom_call_target="tpu_custom_call" | custom-call | flops 2000000000 | bytes 8000000 | tf_op jit(solution)/shard_map/early_pairs/pallas_call | solution.py:710
  16.9 0.0 collective-permute-done.1.far_hbm
  16.9 16.2 %encode.1 = (bf16[48,768]{1,0:T(8,128)(2,1)}, bf16[384,128]{1,0:T(8,128)(2,1)}) custom-call(bf16[784,128]{1,0:T(8,128)(2,1)} %project.1.own_hbm, bf16[784,128]{1,0:T(8,128)(2,1)S(1)} %collective-permute-done.near_hbm, bf16[784,128]{1,0:T(8,128)(2,1)S(1)} %collective-permute-done.1.far_hbm, f32[15,3,128,128]{3,2,1,0:T(8,128)S(1)} %early_pairs.1.early_ref, ...), custom_call_target="tpu_custom_call" | custom-call | tf_op jit(solution)/shard_map/encode/pallas_call | solution.py:722
Async XLA Ops:
  4.8 4.6 %collective-permute-start = (bf16[784,128]{1,0:T(8,128)(2,1)}, bf16[784,128]{1,0:T(8,128)(2,1)S(1)}, u32[]{:S(2)}, u32[]{:S(2)}) collective-permute-start(bf16[784,128]{1,0:T(8,128)(2,1)} %project.1.own_hbm), channel_id=1, source_target_pairs={{0,1},{1,0},{2,3},{3,2},{4,5},{5,4},{6,7},{7,6},{8,9},{9,8},{10,11... | collective-permute-start | bytes 602120 | tf_op jit(solution)/shard_map/ppermute | solution.py:668
  4.9 12.0 %collective-permute-start.1 = (bf16[784,128]{1,0:T(8,128)(2,1)}, bf16[784,128]{1,0:T(8,128)(2,1)S(1)}, u32[]{:S(2)}, u32[]{:S(2)}) collective-permute-start(bf16[784,128]{1,0:T(8,128)(2,1)} %project.1.own_hbm), channel_id=1, source_target_pairs={{1,2},{2,1},{3,4},{4,3},{5,6},{6,5},{7,8},{8,7},{9,10},{10,9},{11,... | collective-permute-start | bytes 602120 | tf_op jit(solution)/shard_map/ppermute | solution.py:669
